TPU v7x, 128 devices: a whole 4x4x4 slice. The times are simulated.
128 devices in a mesh: section: 8 (over y, core), edge: 16 (over z, x).
Axes of the slice: x: 4, y: 4, z: 4, core: 2. Of those that a mesh axis runs over, the one named last changes fastest.
Arguments:
- layer_nodes: bfloat16 [8, 2, 256, 512], P('section'), may hold values from -6 to 6
- layer_edges: bfloat16 [8, 2, 4096, 512], P('section', None, 'edge'), may hold values from -6 to 6
- top_nodes: bfloat16 [2, 256, 512], replicated, may hold values from -1.5 to 1.5
- top_edges: bfloat16 [2, 4096, 512], P(None, 'edge'), may hold values from -1.5 to 1.5
- tile_blocks: int32 [2, 32, 2], P(None, 'edge'), may hold values from 0 to 1
- senders: int32 [2, 4096], P(None, 'edge'), may hold values from 0 to 127
- receivers: int32 [2, 4096], P(None, 'edge'), may hold values from 0 to 127
- w_send: bfloat16 [8, 512, 512], P('section'), may hold values from -0.0625 to 0.0625
- w_recv: bfloat16 [8, 512, 512], P('section'), may hold values from -0.0625 to 0.0625
- w_edge: bfloat16 [8, 512, 512], P('section'), may hold values from -0.25 to 0.25
- w_msg: bfloat16 [8, 512, 512], P('section'), may hold values from -0.125 to 0.125
- w_node: bfloat16 [8, 512, 512], P('section'), may hold values from -0.25 to 0.25
- w_agg: bfloat16 [8, 512, 512], P('section'), may hold values from -0.25 to 0.25
- w_out: bfloat16 [8, 512, 512], P('section'), may hold values from -0.125 to 0.125
Outputs:
- node_grads: bfloat16 [8, 2, 256, 512], P('section', None, 'edge')
- edge_grads: bfloat16 [8, 2, 4096, 512], P('section', None, 'edge')
- g_send: float32 [8, 512, 512], P('section', 'edge')
- g_recv: float32 [8, 512, 512], P('section', 'edge')
- g_edge: float32 [8, 512, 512], P('section', 'edge')
- g_msg: float32 [8, 512, 512], P('section', 'edge')
- g_node: float32 [8, 512, 512], P('section', 'edge')
- g_agg: float32 [8, 512, 512], P('section', 'edge')
- g_out: float32 [8, 512, 512], P('section', 'edge')
All inputs are finite; a program needn't handle non-finite values.
Results may differ from a plain program's by a relative error of at most 0.029.
Values may be sent and summed in bfloat16 or wider, within the bound.
A program may use at most 64 MiB of HBM per device.

v0:
```python
import jax
import jax.numpy as jnp
from jax import lax
from jax.sharding import PartitionSpec as P

BLOCK = 128


def shifted(shard, axis, by):
    peers = lax.axis_size(axis)
    pairs = [(i, i + by) for i in range(peers) if 0 <= i + by < peers]
    return lax.ppermute(shard, axis, pairs)


def silu_slope(values):
    sigma = jax.nn.sigmoid(values)
    return sigma * (1.0 + values * (1.0 - sigma))


def matmul(left, right):
    return jnp.dot(left, right, preferred_element_type=jnp.float32)


def times_transposed(left, right):
    return lax.dot_general(
        left, right, (((1,), (1,)), ((), ())), preferred_element_type=jnp.float32
    )


def transposed_times(left, right):
    return lax.dot_general(
        left, right, (((0,), (0,)), ((), ())), preferred_element_type=jnp.float32
    )


def to_edges(values, block_hot, edge_hot):
    width = values.shape[1]
    grouped = values.reshape(block_hot.shape[1], -1, width)
    picked = jnp.einsum(
        "tb,bcd->tcd", block_hot, grouped, preferred_element_type=jnp.float32
    ).astype(jnp.bfloat16)
    spread = jnp.einsum("tec,tcd->ted", edge_hot, picked, preferred_element_type=jnp.float32)
    return spread.reshape(-1, width).astype(jnp.bfloat16)


def to_nodes(values, block_hot, edge_hot):
    width = values.shape[1]
    per_tile = jnp.einsum(
        "tec,ted->tcd",
        edge_hot,
        values.reshape(block_hot.shape[0], -1, width),
        preferred_element_type=jnp.float32,
    )
    summed = jnp.einsum(
        "tb,tcd->bcd", block_hot.astype(jnp.float32), per_tile, precision=lax.Precision.HIGHEST
    )
    return summed.reshape(-1, width)


def body(
    layer_nodes,
    layer_edges,
    top_nodes,
    top_edges,
    tile_blocks,
    senders,
    receivers,
    w_send,
    w_recv,
    w_edge,
    w_msg,
    w_node,
    w_agg,
    w_out,
):
    sections = lax.axis_size("section")
    section = lax.axis_index("section")
    groups = lax.axis_size("edge")
    member = lax.axis_index("edge")
    nodes_all = layer_nodes[0]
    edges_all = layer_edges[0]
    batches = nodes_all.shape[0]
    node_count = nodes_all.shape[1]
    width = nodes_all.shape[2]
    tile_count = tile_blocks.shape[1]
    tile_len = edges_all.shape[1] // tile_count
    block_count = node_count // BLOCK
    row_count = node_count // groups
    weight_send, weight_recv, weight_edge, weight_msg = (w_send[0], w_recv[0], w_edge[0], w_msg[0])
    weight_node, weight_agg, weight_out = (w_node[0], w_agg[0], w_out[0])
    lanes = jnp.arange(BLOCK, dtype=jnp.int32)
    slots = jnp.arange(block_count, dtype=jnp.int32)
    send_hot = (senders.reshape(batches, tile_count, tile_len)[..., None] == lanes).astype(
        jnp.bfloat16
    )
    recv_hot = (receivers.reshape(batches, tile_count, tile_len)[..., None] == lanes).astype(
        jnp.bfloat16
    )
    send_block = (tile_blocks[:, :, 0][..., None] == slots).astype(jnp.bfloat16)
    recv_block = (tile_blocks[:, :, 1][..., None] == slots).astype(jnp.bfloat16)

    def advance(moment, carry):
        node_in_grad, edge_in_grad, totals, node_record, edge_record = carry
        batch_raw = moment - (sections - 1 - section)
        valid = (batch_raw >= 0) & (batch_raw < batches)
        batch = jnp.clip(batch_raw, 0, batches - 1)
        feats = lax.dynamic_index_in_dim(nodes_all, batch, 0, keepdims=False)
        edge_feats = lax.dynamic_index_in_dim(edges_all, batch, 0, keepdims=False)
        send_tiles = lax.dynamic_index_in_dim(send_hot, batch, 0, keepdims=False)
        recv_tiles = lax.dynamic_index_in_dim(recv_hot, batch, 0, keepdims=False)
        send_blocks = lax.dynamic_index_in_dim(send_block, batch, 0, keepdims=False)
        recv_blocks = lax.dynamic_index_in_dim(recv_block, batch, 0, keepdims=False)
        top_node = lax.dynamic_index_in_dim(top_nodes, batch, 0, keepdims=False)
        top_edge = lax.dynamic_index_in_dim(top_edges, batch, 0, keepdims=False)
        is_last = section == sections - 1
        grad_nodes = jnp.where(is_last, top_node, node_in_grad)
        grad_edges = jnp.where(is_last, top_edge, edge_in_grad)
        send_feats = to_edges(feats, send_blocks, send_tiles)
        recv_feats = to_edges(feats, recv_blocks, recv_tiles)
        pre = (
            matmul(send_feats, weight_send)
            + matmul(recv_feats, weight_recv)
            + matmul(edge_feats, weight_edge)
        )
        act = jax.nn.silu(pre).astype(jnp.bfloat16)
        message = matmul(act, weight_msg).astype(jnp.bfloat16)
        partial_agg = to_nodes(message, recv_blocks, recv_tiles)
        aggregate = lax.psum(partial_agg, "edge")
        agg_b = aggregate.astype(jnp.bfloat16)
        node_pre = matmul(feats, weight_node) + matmul(agg_b, weight_agg)
        node_act = jax.nn.silu(node_pre).astype(jnp.bfloat16)
        node_delta = (times_transposed(grad_nodes, weight_out) * silu_slope(node_pre)).astype(
            jnp.bfloat16
        )
        agg_grad = times_transposed(node_delta, weight_agg).astype(jnp.bfloat16)
        node_term = times_transposed(node_delta, weight_node)
        agg_edges = to_edges(agg_grad, recv_blocks, recv_tiles)
        message_grad = (grad_edges.astype(jnp.float32) + agg_edges.astype(jnp.float32)).astype(
            jnp.bfloat16
        )
        edge_delta = (times_transposed(message_grad, weight_msg) * silu_slope(pre)).astype(
            jnp.bfloat16
        )
        edge_out = (
            grad_edges.astype(jnp.float32) + times_transposed(edge_delta, weight_edge)
        ).astype(jnp.bfloat16)
        send_grad = times_transposed(edge_delta, weight_send).astype(jnp.bfloat16)
        recv_grad = times_transposed(edge_delta, weight_recv).astype(jnp.bfloat16)
        partial_back = to_nodes(send_grad, send_blocks, send_tiles) + to_nodes(
            recv_grad, recv_blocks, recv_tiles
        )
        edge_terms = lax.psum(partial_back, "edge")
        node_out = (grad_nodes.astype(jnp.float32) + node_term + edge_terms).astype(jnp.bfloat16)
        fresh = (
            transposed_times(send_feats, edge_delta),
            transposed_times(recv_feats, edge_delta),
            transposed_times(edge_feats, edge_delta),
            transposed_times(act, message_grad),
            transposed_times(feats, node_delta),
            transposed_times(agg_b, node_delta),
            transposed_times(node_act, grad_nodes),
        )
        totals = tuple(
            (jnp.where(valid, before + extra, before) for before, extra in zip(totals, fresh))
        )
        own_out = lax.dynamic_slice_in_dim(node_out, member * row_count, row_count, 0)
        node_record = jnp.where(
            valid, lax.dynamic_update_index_in_dim(node_record, own_out, batch, 0), node_record
        )
        edge_record = jnp.where(
            valid, lax.dynamic_update_index_in_dim(edge_record, edge_out, batch, 0), edge_record
        )
        sent_nodes, sent_edges = shifted((node_out, edge_out), "section", -1)
        return (sent_nodes, sent_edges, totals, node_record, edge_record)

    hidden = weight_send.shape[1]
    square_in = jnp.zeros((width, hidden), jnp.float32)
    square_back = jnp.zeros((hidden, width), jnp.float32)
    start = (
        jnp.zeros((node_count, width), jnp.bfloat16),
        jnp.zeros(edges_all.shape[1:], jnp.bfloat16),
        (square_in, square_in, square_in, square_back, square_in, square_in, square_back),
        jnp.zeros((batches, row_count, width), jnp.bfloat16),
        jnp.zeros(edges_all.shape, jnp.bfloat16),
    )
    finished = lax.fori_loop(0, sections + batches - 1, advance, start)
    totals, node_record, edge_record = (finished[2], finished[3], finished[4])
    sum_send, sum_recv, sum_edge, sum_msg, sum_node, sum_agg, sum_out = totals
    sum_send, sum_recv, sum_edge, sum_msg = (
        lax.psum_scatter(sum_send, "edge", scatter_dimension=0, tiled=True),
        lax.psum_scatter(sum_recv, "edge", scatter_dimension=0, tiled=True),
        lax.psum_scatter(sum_edge, "edge", scatter_dimension=0, tiled=True),
        lax.psum_scatter(sum_msg, "edge", scatter_dimension=0, tiled=True),
    )
    sum_node = lax.dynamic_slice_in_dim(sum_node, member * (width // groups), width // groups, 0)
    sum_agg = lax.dynamic_slice_in_dim(sum_agg, member * (width // groups), width // groups, 0)
    sum_out = lax.dynamic_slice_in_dim(sum_out, member * (hidden // groups), hidden // groups, 0)
    return (
        node_record[None],
        edge_record[None],
        sum_send[None],
        sum_recv[None],
        sum_edge[None],
        sum_msg[None],
        sum_node[None],
        sum_agg[None],
        sum_out[None],
    )


def solution(mesh):
    in_specs = (
        P("section", None, None, None),
        P("section", None, "edge", None),
        P(),
        P(None, "edge", None),
        P(None, "edge", None),
        P(None, "edge"),
        P(None, "edge"),
        P("section", None, None),
        P("section", None, None),
        P("section", None, None),
        P("section", None, None),
        P("section", None, None),
        P("section", None, None),
        P("section", None, None),
    )
    out_specs = (
        P("section", None, "edge", None),
        P("section", None, "edge", None),
        P("section", "edge", None),
        P("section", "edge", None),
        P("section", "edge", None),
        P("section", "edge", None),
        P("section", "edge", None),
        P("section", "edge", None),
        P("section", "edge", None),
    )
    return jax.shard_map(body, mesh=mesh, in_specs=in_specs, out_specs=out_specs, check_vma=False)
```

profile of v0, /device:TPU:0, one launch (start us, length us, event | category | flops | bytes accessed | tf_op | source)
XLA Modules:
  0.0 2031.3 jit_solution(16253940211328947030)
XLA Ops:
  13.3 1701.8 %while.36 = (s32[]{:T(128)}, bf16[256,512]{1,0:T(8,128)(2,1)S(1)}, bf16[256,512]{1,0:T(8,128)(2,1)S(1)}, f32[512,512]{1,0:T(8,128)}, f32[512,512]{1,0:T(8,128)},...) while((s32[]{:T(128)}, bf16[256,512]{1,0:T(8,128)(2,1)S(1)}, ...), condition=%wide.region_3.4_spmd.clone, body=%wide.region_0.3_spmd.clone.sunk | while | flops 2910199808 | bytes 137546704 | solution.py:186
  21.1 81.4 %all-reduce.4 = bf16[256,512]{1,0:T(8,128)(2,1)S(1)} all-reduce(f32[256,512]{1,0:T(8,128)S(1)} %bitcast.271), channel_id=1, replica_groups=mesh['section'=8,'edge'=16] {'edge'}, use_global_device_ids=true, to_apply=%region_1.1 | all-reduce | flops 131072 | bytes 786432 | tf_op jit(solution)/shard_map/while/body/eval_jaxpr/psum | solution.py:128
  116.8 2.2 fusion.248
  120.3 2.6 add_select_fusion.17
  129.5 69.2 %all-reduce.3.cloned.1.call-done = f32[256,512]{1,0:T(8,128)} async-done(((f32[256,512]{1,0:T(8,128)}), f32[256,512]{1,0:T(8,128)}) %all-reduce.3.cloned.1.call-update) | async-done | bytes 524304 | tf_op jit(solution)/shard_map/while/body/eval_jaxpr/psum | solution.py:152
  211.4 77.6 %all-reduce.4 = bf16[256,512]{1,0:T(8,128)(2,1)S(1)} all-reduce(f32[256,512]{1,0:T(8,128)S(1)} %bitcast.271), channel_id=1, replica_groups=mesh['section'=8,'edge'=16] {'edge'}, use_global_device_ids=true, to_apply=%region_1.1 | all-reduce | flops 131072 | bytes 786432 | tf_op jit(solution)/shard_map/while/body/eval_jaxpr/psum | solution.py:128
  303.3 2.2 fusion.248
  306.7 2.9 add_select_fusion.17
  314.9 2.6 add_select_fusion.20
  317.5 70.1 %all-reduce.3.cloned.1.call-done = f32[256,512]{1,0:T(8,128)} async-done(((f32[256,512]{1,0:T(8,128)}), f32[256,512]{1,0:T(8,128)}) %all-reduce.3.cloned.1.call-update) | async-done | bytes 524304 | tf_op jit(solution)/shard_map/while/body/eval_jaxpr/psum | solution.py:152
  400.3 77.6 %all-reduce.4 = bf16[256,512]{1,0:T(8,128)(2,1)S(1)} all-reduce(f32[256,512]{1,0:T(8,128)S(1)} %bitcast.271), channel_id=1, replica_groups=mesh['section'=8,'edge'=16] {'edge'}, use_global_device_ids=true, to_apply=%region_1.1 | all-reduce | flops 131072 | bytes 786432 | tf_op jit(solution)/shard_map/while/body/eval_jaxpr/psum | solution.py:128
  492.2 2.2 fusion.248
  495.7 2.9 add_select_fusion.17
  503.9 2.6 add_select_fusion.20
  506.5 70.1 %all-reduce.3.cloned.1.call-done = f32[256,512]{1,0:T(8,128)} async-done(((f32[256,512]{1,0:T(8,128)}), f32[256,512]{1,0:T(8,128)}) %all-reduce.3.cloned.1.call-update) | async-done | bytes 524304 | tf_op jit(solution)/shard_map/while/body/eval_jaxpr/psum | solution.py:152
  589.3 77.6 %all-reduce.4 = bf16[256,512]{1,0:T(8,128)(2,1)S(1)} all-reduce(f32[256,512]{1,0:T(8,128)S(1)} %bitcast.271), channel_id=1, replica_groups=mesh['section'=8,'edge'=16] {'edge'}, use_global_device_ids=true, to_apply=%region_1.1 | all-reduce | flops 131072 | bytes 786432 | tf_op jit(solution)/shard_map/while/body/eval_jaxpr/psum | solution.py:128
  681.2 2.2 fusion.248
  684.6 2.9 add_select_fusion.17
  692.8 2.6 add_select_fusion.20
  695.4 70.1 %all-reduce.3.cloned.1.call-done = f32[256,512]{1,0:T(8,128)} async-done(((f32[256,512]{1,0:T(8,128)}), f32[256,512]{1,0:T(8,128)}) %all-reduce.3.cloned.1.call-update) | async-done | bytes 524304 | tf_op jit(solution)/shard_map/while/body/eval_jaxpr/psum | solution.py:152
  778.2 77.6 %all-reduce.4 = bf16[256,512]{1,0:T(8,128)(2,1)S(1)} all-reduce(f32[256,512]{1,0:T(8,128)S(1)} %bitcast.271), channel_id=1, replica_groups=mesh['section'=8,'edge'=16] {'edge'}, use_global_device_ids=true, to_apply=%region_1.1 | all-reduce | flops 131072 | bytes 786432 | tf_op jit(solution)/shard_map/while/body/eval_jaxpr/psum | solution.py:128
  870.1 2.2 fusion.248
  873.6 2.9 add_select_fusion.17
  881.8 2.6 add_select_fusion.20
  884.4 70.1 %all-reduce.3.cloned.1.call-done = f32[256,512]{1,0:T(8,128)} async-done(((f32[256,512]{1,0:T(8,128)}), f32[256,512]{1,0:T(8,128)}) %all-reduce.3.cloned.1.call-update) | async-done | bytes 524304 | tf_op jit(solution)/shard_map/while/body/eval_jaxpr/psum | solution.py:152
  967.2 77.6 %all-reduce.4 = bf16[256,512]{1,0:T(8,128)(2,1)S(1)} all-reduce(f32[256,512]{1,0:T(8,128)S(1)} %bitcast.271), channel_id=1, replica_groups=mesh['section'=8,'edge'=16] {'edge'}, use_global_device_ids=true, to_apply=%region_1.1 | all-reduce | flops 131072 | bytes 786432 | tf_op jit(solution)/shard_map/while/body/eval_jaxpr/psum | solution.py:128
  1059.1 2.2 fusion.248
  1062.5 2.9 add_select_fusion.17
  1070.7 2.6 add_select_fusion.20
  1073.3 70.1 %all-reduce.3.cloned.1.call-done = f32[256,512]{1,0:T(8,128)} async-done(((f32[256,512]{1,0:T(8,128)}), f32[256,512]{1,0:T(8,128)}) %all-reduce.3.cloned.1.call-update) | async-done | bytes 524304 | tf_op jit(solution)/shard_map/while/body/eval_jaxpr/psum | solution.py:152
  1156.1 77.6 %all-reduce.4 = bf16[256,512]{1,0:T(8,128)(2,1)S(1)} all-reduce(f32[256,512]{1,0:T(8,128)S(1)} %bitcast.271), channel_id=1, replica_groups=mesh['section'=8,'edge'=16] {'edge'}, use_global_device_ids=true, to_apply=%region_1.1 | all-reduce | flops 131072 | bytes 786432 | tf_op jit(solution)/shard_map/while/body/eval_jaxpr/psum | solution.py:128
  1251.5 2.9 add_select_fusion.17
  1259.7 2.6 add_select_fusion.20
  1262.3 70.1 %all-reduce.3.cloned.1.call-done = f32[256,512]{1,0:T(8,128)} async-done(((f32[256,512]{1,0:T(8,128)}), f32[256,512]{1,0:T(8,128)}) %all-reduce.3.cloned.1.call-update) | async-done | bytes 524304 | tf_op jit(solution)/shard_map/while/body/eval_jaxpr/psum | solution.py:152
  1345.1 77.6 %all-reduce.4 = bf16[256,512]{1,0:T(8,128)(2,1)S(1)} all-reduce(f32[256,512]{1,0:T(8,128)S(1)} %bitcast.271), channel_id=1, replica_groups=mesh['section'=8,'edge'=16] {'edge'}, use_global_device_ids=true, to_apply=%region_1.1 | all-reduce | flops 131072 | bytes 786432 | tf_op jit(solution)/shard_map/while/body/eval_jaxpr/psum | solution.py:128
  1437.0 2.2 fusion.248
  1440.4 2.9 add_select_fusion.17
  1448.6 2.6 add_select_fusion.20
  1451.2 70.1 %all-reduce.3.cloned.1.call-done = f32[256,512]{1,0:T(8,128)} async-done(((f32[256,512]{1,0:T(8,128)}), f32[256,512]{1,0:T(8,128)}) %all-reduce.3.cloned.1.call-update) | async-done | bytes 524304 | tf_op jit(solution)/shard_map/while/body/eval_jaxpr/psum | solution.py:152
  1534.1 77.6 %all-reduce.4 = bf16[256,512]{1,0:T(8,128)(2,1)S(1)} all-reduce(f32[256,512]{1,0:T(8,128)S(1)} %bitcast.271), channel_id=1, replica_groups=mesh['section'=8,'edge'=16] {'edge'}, use_global_device_ids=true, to_apply=%region_1.1 | all-reduce | flops 131072 | bytes 786432 | tf_op jit(solution)/shard_map/while/body/eval_jaxpr/psum | solution.py:128
  1625.9 2.2 fusion.248
  1629.4 2.9 add_select_fusion.17
  1637.6 2.6 add_select_fusion.20
  1640.2 70.1 %all-reduce.3.cloned.1.call-done = f32[256,512]{1,0:T(8,128)} async-done(((f32[256,512]{1,0:T(8,128)}), f32[256,512]{1,0:T(8,128)}) %all-reduce.3.cloned.1.call-update) | async-done | bytes 524304 | tf_op jit(solution)/shard_map/while/body/eval_jaxpr/psum | solution.py:152
  1722.0 73.1 %reduce-scatter.5.cloned.1.call-done = f32[32,512]{1,0:T(8,128)} async-done(((f32[512,512]{1,0:T(8,128)}), f32[32,512]{1,0:T(8,128)}) %reduce-scatter.5.cloned.1.call-update) | async-done | bytes 65552 | tf_op jit(solution)/shard_map/reduce_scatter | solution.py:190
  1795.1 76.3 %reduce-scatter.7.cloned.1.call-done = f32[32,512]{1,0:T(8,128)} async-done(((f32[512,512]{1,0:T(8,128)}), f32[32,512]{1,0:T(8,128)}) %reduce-scatter.7.cloned.1.call-update) | async-done | bytes 65552 | tf_op jit(solution)/shard_map/reduce_scatter | solution.py:191
  1871.4 76.0 %reduce-scatter.9.cloned.1.call-done = f32[32,512]{1,0:T(8,128)} async-done(((f32[512,512]{1,0:T(8,128)}), f32[32,512]{1,0:T(8,128)}) %reduce-scatter.9.cloned.1.call-update) | async-done | bytes 65552 | tf_op jit(solution)/shard_map/reduce_scatter | solution.py:192
  1947.4 76.5 %reduce-scatter.11.cloned.1.call-done = f32[32,512]{1,0:T(8,128)} async-done(((f32[512,512]{1,0:T(8,128)}), f32[32,512]{1,0:T(8,128)}) %reduce-scatter.11.cloned.1.call-update) | async-done | bytes 65552 | tf_op jit(solution)/shard_map/reduce_scatter | solution.py:193
  (975 shorter events, 313.7 us)
Async XLA Ops:
  13.3 185.4 %all-reduce.3.cloned.1.call-start = ((), (), s32[]{:S(2)}) async-start(), calls=%async_computation.8 | async-start | bytes 1048576 | tf_op jit(solution)/shard_map/while/body/eval_jaxpr/psum | solution.py:152
  119.0 83.2 %collective-permute-start.1 = (bf16[256,512]{1,0:T(8,128)(2,1)}, bf16[256,512]{1,0:T(8,128)(2,1)S(1)}, u32[]{:S(2)}, u32[]{:S(2)}) collective-permute-start(bf16[256,512]{1,0:T(8,128)(2,1)} %get-tuple-element.1012), channel_id=1, source_target_pairs={{16,0},{32,16},{48,32},{64,48},{80,64},{96,80},{112,96},{17,1},{33... | collective-permute-start | bytes 786440 | tf_op jit(solution)/shard_map/while/body/eval_jaxpr/ppermute | solution.py:12
  129.4 71.9 %copy-start.11 = (f32[512,512]{1,0:T(8,128)S(1)}, f32[512,512]{1,0:T(8,128)}, u32[]{:S(2)}) copy-start(f32[512,512]{1,0:T(8,128)} %get-tuple-element.1052) | copy-start | bytes 3145732 | tf_op jit(solution)/shard_map/while
  200.1 3.4 collective-permute-start
  203.5 184.1 %all-reduce.3.cloned.1.call-start = ((), (), s32[]{:S(2)}) async-start(), calls=%async_computation.8 | async-start | bytes 1048576 | tf_op jit(solution)/shard_map/while/body/eval_jaxpr/psum | solution.py:152
  305.4 85.7 %collective-permute-start.1 = (bf16[256,512]{1,0:T(8,128)(2,1)}, bf16[256,512]{1,0:T(8,128)(2,1)S(1)}, u32[]{:S(2)}, u32[]{:S(2)}) collective-permute-start(bf16[256,512]{1,0:T(8,128)(2,1)} %get-tuple-element.1012), channel_id=1, source_target_pairs={{16,0},{32,16},{48,32},{64,48},{80,64},{96,80},{112,96},{17,1},{33... | collective-permute-start | bytes 786440 | tf_op jit(solution)/shard_map/while/body/eval_jaxpr/ppermute | solution.py:12
  306.7 2.9 copy-start.7
  317.5 72.8 %copy-start.11 = (f32[512,512]{1,0:T(8,128)S(1)}, f32[512,512]{1,0:T(8,128)}, u32[]{:S(2)}) copy-start(f32[512,512]{1,0:T(8,128)} %get-tuple-element.1052) | copy-start | bytes 3145732 | tf_op jit(solution)/shard_map/while
  389.0 3.4 collective-permute-start
  392.5 184.1 %all-reduce.3.cloned.1.call-start = ((), (), s32[]{:S(2)}) async-start(), calls=%async_computation.8 | async-start | bytes 1048576 | tf_op jit(solution)/shard_map/while/body/eval_jaxpr/psum | solution.py:152
  494.4 85.7 %collective-permute-start.1 = (bf16[256,512]{1,0:T(8,128)(2,1)}, bf16[256,512]{1,0:T(8,128)(2,1)S(1)}, u32[]{:S(2)}, u32[]{:S(2)}) collective-permute-start(bf16[256,512]{1,0:T(8,128)(2,1)} %get-tuple-element.1012), channel_id=1, source_target_pairs={{16,0},{32,16},{48,32},{64,48},{80,64},{96,80},{112,96},{17,1},{33... | collective-permute-start | bytes 786440 | tf_op jit(solution)/shard_map/while/body/eval_jaxpr/ppermute | solution.py:12
  495.7 2.9 copy-start.7
  506.5 72.8 %copy-start.11 = (f32[512,512]{1,0:T(8,128)S(1)}, f32[512,512]{1,0:T(8,128)}, u32[]{:S(2)}) copy-start(f32[512,512]{1,0:T(8,128)} %get-tuple-element.1052) | copy-start | bytes 3145732 | tf_op jit(solution)/shard_map/while
  578.0 3.4 collective-permute-start
  581.4 184.1 %all-reduce.3.cloned.1.call-start = ((), (), s32[]{:S(2)}) async-start(), calls=%async_computation.8 | async-start | bytes 1048576 | tf_op jit(solution)/shard_map/while/body/eval_jaxpr/psum | solution.py:152
  683.3 85.7 %collective-permute-start.1 = (bf16[256,512]{1,0:T(8,128)(2,1)}, bf16[256,512]{1,0:T(8,128)(2,1)S(1)}, u32[]{:S(2)}, u32[]{:S(2)}) collective-permute-start(bf16[256,512]{1,0:T(8,128)(2,1)} %get-tuple-element.1012), channel_id=1, source_target_pairs={{16,0},{32,16},{48,32},{64,48},{80,64},{96,80},{112,96},{17,1},{33... | collective-permute-start | bytes 786440 | tf_op jit(solution)/shard_map/while/body/eval_jaxpr/ppermute | solution.py:12
  684.6 2.9 copy-start.7
  695.4 72.8 %copy-start.11 = (f32[512,512]{1,0:T(8,128)S(1)}, f32[512,512]{1,0:T(8,128)}, u32[]{:S(2)}) copy-start(f32[512,512]{1,0:T(8,128)} %get-tuple-element.1052) | copy-start | bytes 3145732 | tf_op jit(solution)/shard_map/while
  766.9 3.4 collective-permute-start
  770.4 184.1 %all-reduce.3.cloned.1.call-start = ((), (), s32[]{:S(2)}) async-start(), calls=%async_computation.8 | async-start | bytes 1048576 | tf_op jit(solution)/shard_map/while/body/eval_jaxpr/psum | solution.py:152
  872.3 85.7 %collective-permute-start.1 = (bf16[256,512]{1,0:T(8,128)(2,1)}, bf16[256,512]{1,0:T(8,128)(2,1)S(1)}, u32[]{:S(2)}, u32[]{:S(2)}) collective-permute-start(bf16[256,512]{1,0:T(8,128)(2,1)} %get-tuple-element.1012), channel_id=1, source_target_pairs={{16,0},{32,16},{48,32},{64,48},{80,64},{96,80},{112,96},{17,1},{33... | collective-permute-start | bytes 786440 | tf_op jit(solution)/shard_map/while/body/eval_jaxpr/ppermute | solution.py:12
  873.6 2.9 copy-start.7
  884.4 72.8 %copy-start.11 = (f32[512,512]{1,0:T(8,128)S(1)}, f32[512,512]{1,0:T(8,128)}, u32[]{:S(2)}) copy-start(f32[512,512]{1,0:T(8,128)} %get-tuple-element.1052) | copy-start | bytes 3145732 | tf_op jit(solution)/shard_map/while
  955.9 3.4 collective-permute-start
  959.3 184.1 %all-reduce.3.cloned.1.call-start = ((), (), s32[]{:S(2)}) async-start(), calls=%async_computation.8 | async-start | bytes 1048576 | tf_op jit(solution)/shard_map/while/body/eval_jaxpr/psum | solution.py:152
  1061.2 85.7 %collective-permute-start.1 = (bf16[256,512]{1,0:T(8,128)(2,1)}, bf16[256,512]{1,0:T(8,128)(2,1)S(1)}, u32[]{:S(2)}, u32[]{:S(2)}) collective-permute-start(bf16[256,512]{1,0:T(8,128)(2,1)} %get-tuple-element.1012), channel_id=1, source_target_pairs={{16,0},{32,16},{48,32},{64,48},{80,64},{96,80},{112,96},{17,1},{33... | collective-permute-start | bytes 786440 | tf_op jit(solution)/shard_map/while/body/eval_jaxpr/ppermute | solution.py:12
  1062.5 2.9 copy-start.7
  1073.3 72.8 %copy-start.11 = (f32[512,512]{1,0:T(8,128)S(1)}, f32[512,512]{1,0:T(8,128)}, u32[]{:S(2)}) copy-start(f32[512,512]{1,0:T(8,128)} %get-tuple-element.1052) | copy-start | bytes 3145732 | tf_op jit(solution)/shard_map/while
  1144.8 3.4 collective-permute-start
  1148.3 184.1 %all-reduce.3.cloned.1.call-start = ((), (), s32[]{:S(2)}) async-start(), calls=%async_computation.8 | async-start | bytes 1048576 | tf_op jit(solution)/shard_map/while/body/eval_jaxpr/psum | solution.py:152
  1250.2 85.7 %collective-permute-start.1 = (bf16[256,512]{1,0:T(8,128)(2,1)}, bf16[256,512]{1,0:T(8,128)(2,1)S(1)}, u32[]{:S(2)}, u32[]{:S(2)}) collective-permute-start(bf16[256,512]{1,0:T(8,128)(2,1)} %get-tuple-element.1012), channel_id=1, source_target_pairs={{16,0},{32,16},{48,32},{64,48},{80,64},{96,80},{112,96},{17,1},{33... | collective-permute-start | bytes 786440 | tf_op jit(solution)/shard_map/while/body/eval_jaxpr/ppermute | solution.py:12
  1251.5 2.9 copy-start.7
  1262.3 72.8 %copy-start.11 = (f32[512,512]{1,0:T(8,128)S(1)}, f32[512,512]{1,0:T(8,128)}, u32[]{:S(2)}) copy-start(f32[512,512]{1,0:T(8,128)} %get-tuple-element.1052) | copy-start | bytes 3145732 | tf_op jit(solution)/shard_map/while
  1333.8 3.4 collective-permute-start
  1337.2 184.1 %all-reduce.3.cloned.1.call-start = ((), (), s32[]{:S(2)}) async-start(), calls=%async_computation.8 | async-start | bytes 1048576 | tf_op jit(solution)/shard_map/while/body/eval_jaxpr/psum | solution.py:152
  1439.1 85.7 %collective-permute-start.1 = (bf16[256,512]{1,0:T(8,128)(2,1)}, bf16[256,512]{1,0:T(8,128)(2,1)S(1)}, u32[]{:S(2)}, u32[]{:S(2)}) collective-permute-start(bf16[256,512]{1,0:T(8,128)(2,1)} %get-tuple-element.1012), channel_id=1, source_target_pairs={{16,0},{32,16},{48,32},{64,48},{80,64},{96,80},{112,96},{17,1},{33... | collective-permute-start | bytes 786440 | tf_op jit(solution)/shard_map/while/body/eval_jaxpr/ppermute | solution.py:12
  1440.4 2.9 copy-start.7
  1451.2 72.8 %copy-start.11 = (f32[512,512]{1,0:T(8,128)S(1)}, f32[512,512]{1,0:T(8,128)}, u32[]{:S(2)}) copy-start(f32[512,512]{1,0:T(8,128)} %get-tuple-element.1052) | copy-start | bytes 3145732 | tf_op jit(solution)/shard_map/while
  1522.7 3.4 collective-permute-start
  1526.2 184.1 %all-reduce.3.cloned.1.call-start = ((), (), s32[]{:S(2)}) async-start(), calls=%async_computation.8 | async-start | bytes 1048576 | tf_op jit(solution)/shard_map/while/body/eval_jaxpr/psum | solution.py:152
  1628.1 85.7 %collective-permute-start.1 = (bf16[256,512]{1,0:T(8,128)(2,1)}, bf16[256,512]{1,0:T(8,128)(2,1)S(1)}, u32[]{:S(2)}, u32[]{:S(2)}) collective-permute-start(bf16[256,512]{1,0:T(8,128)(2,1)} %get-tuple-element.1012), channel_id=1, source_target_pairs={{16,0},{32,16},{48,32},{64,48},{80,64},{96,80},{112,96},{17,1},{33... | collective-permute-start | bytes 786440 | tf_op jit(solution)/shard_map/while/body/eval_jaxpr/ppermute | solution.py:12
  1629.4 2.9 copy-start.7
  1640.2 72.8 %copy-start.11 = (f32[512,512]{1,0:T(8,128)S(1)}, f32[512,512]{1,0:T(8,128)}, u32[]{:S(2)}) copy-start(f32[512,512]{1,0:T(8,128)} %get-tuple-element.1052) | copy-start | bytes 3145732 | tf_op jit(solution)/shard_map/while
  1711.7 3.4 collective-permute-start
  1715.1 80.0 %reduce-scatter.5.cloned.1.call-start = ((), (), s32[]{:S(2)}) async-start(), calls=%async_computation.4 | async-start | bytes 1114112 | tf_op jit(solution)/shard_map/reduce_scatter | solution.py:190
  1715.7 155.7 %reduce-scatter.7.cloned.1.call-start = ((), (), s32[]{:S(2)}) async-start(), calls=%async_computation.5 | async-start | bytes 1114112 | tf_op jit(solution)/shard_map/reduce_scatter | solution.py:191
  1716.3 231.1 %reduce-scatter.9.cloned.1.call-start = ((), (), s32[]{:S(2)}) async-start(), calls=%async_computation.6 | async-start | bytes 1114112 | tf_op jit(solution)/shard_map/reduce_scatter | solution.py:192
  1716.9 307.1 %reduce-scatter.11.cloned.1.call-start = ((), (), s32[]{:S(2)}) async-start(), calls=%async_computation.7 | async-start | bytes 1114112 | tf_op jit(solution)/shard_map/reduce_scatter | solution.py:193
  (267 other events, 320.2 us)
Sparse Core Ops, SparseCore 0:
  115.9 82.6 all-reduce.2
  302.4 85.1 all-reduce.2
  491.3 85.1 all-reduce.2
  680.3 85.1 all-reduce.2
  869.2 85.1 all-reduce.2
  1058.2 85.1 all-reduce.2
  1247.1 85.1 all-reduce.2
  1436.1 85.1 all-reduce.2
  1625.0 85.1 all-reduce.2
Sparse Core Ops, SparseCore 1:
  1719.4 75.7 reduce-scatter.4
  1799.1 72.2 reduce-scatter.6
  1875.0 72.3 reduce-scatter.8
  1951.5 72.4 reduce-scatter.10
where the time goes:
time: 2040 us; the launch traced here: 2030 us
  waiting for transfers between devices  946 us (46%)
  blocking collectives  702 us (34%)
  matrix products  214 us (10%)
  local copies, waits for them, and re-layouts  123 us (6%)
  starting transfers between devices  23.3 us (1%)
    psum x9, blocking collectives, advance(): aggregate = lax.psum(partial_agg, 'edge')  702 us
    psum x9, waiting for transfers between devices, advance(): edge_terms = lax.psum(partial_back, 'edge')  630 us
    while x558, local copies, waits for them, and re-layouts  96.3 us
    reduce_scatter x1, waiting for transfers between devices, body(): lax.psum_scatter(sum_msg, 'edge', scatter_dimension=0, tiled=True)  76.5 us
    reduce_scatter x1, waiting for transfers between devices, body(): lax.psum_scatter(sum_recv, 'edge', scatter_dimension=0, tiled=True)  76.3 us
    reduce_scatter x1, waiting for transfers between devices, body(): lax.psum_scatter(sum_edge, 'edge', scatter_dimension=0, tiled=True)  76 us
    reduce_scatter x1, waiting for transfers between devices, body(): lax.psum_scatter(sum_send, 'edge', scatter_dimension=0, tiled=True)  73.1 us
    dot_general x63, matrix products, transposed_times(): lax.dot_general(left, right, (((0,), (0,)), ((), ())), preferred_element_...  70.9 us
  transfers between devices with their start and end apart: 31, of which 22 were waited for; matrix products, arithmetic and copies ran while one was open for 5% of the time, Pallas kernels for 0%

commit v1 on v0

v1 whole, which is shorter than its diff:
```python
import functools

import jax
import jax.numpy as jnp
from jax import lax
from jax.experimental import pallas as pl
from jax.experimental.pallas import tpu as pltpu
from jax.sharding import PartitionSpec as P

MESH = pl.DeviceIdType.MESH
BF = jnp.bfloat16
F32 = jnp.float32


def dot(left, right):
    return jnp.dot(left, right, preferred_element_type=F32)


def dot_t(left, right):
    return lax.dot_general(left, right, (((1,), (1,)), ((), ())), preferred_element_type=F32)


def take_bytes(ref, sem):
    pltpu.make_async_copy(ref, ref, sem).wait()


def kernel(
    sections,
    groups,
    nodes,
    edges,
    top_n,
    top_e,
    blocks,
    senders,
    receivers,
    w_send,
    w_recv,
    w_edge,
    w_msg,
    w_node,
    w_agg,
    w_out,
    node_out,
    edge_out,
    o_send,
    o_recv,
    o_edge,
    o_msg,
    o_node,
    o_agg,
    o_out,
    send_t,
    recv_t,
    recv_1,
    act,
    slope_e,
    slope_n,
    node_delta,
    base,
    w_am,
    nodes_t,
    edges_t,
    act_t,
    agg_t,
    node_act_t,
    total,
    agg_src,
    agg_buf,
    agg_row,
    agg_all,
    back_src,
    back_buf,
    row_src,
    gh,
    ge,
    grad_src,
    grad_buf,
    s_agg,
    r_agg,
    s_all,
    r_all,
    s_back,
    r_back,
    s_gh,
    r_gh,
    s_ge,
    r_ge,
    s_grad,
    r_grad,
):
    section = lax.axis_index("section")
    me = lax.axis_index("edge")
    batches, count, width = nodes.shape
    local = edges.shape[1]
    rows = count // groups
    share = width // groups
    first = section == sections - 1
    last = section == 0

    barrier = pltpu.get_barrier_semaphore()

    def greet(k, carry):
        pl.semaphore_signal(
            barrier, inc=1, device_id=(section, lax.rem(me + k, groups)), device_id_type=MESH
        )
        return carry

    lax.fori_loop(1, groups, greet, 0)

    @pl.when(section < sections - 1)
    def _():
        def greet_up(k, carry):
            pl.semaphore_signal(barrier, inc=1, device_id=(section + 1, k), device_id_type=MESH)
            return carry

        lax.fori_loop(0, groups, greet_up, 0)

    def scatter(src, dst, ssem, rsem):
        def one(k, carry):
            peer = lax.rem(me + k, groups)
            pltpu.make_async_remote_copy(
                src_ref=src.at[peer],
                dst_ref=dst.at[me],
                send_sem=ssem,
                recv_sem=rsem,
                device_id=(section, peer),
                device_id_type=MESH,
            ).start()
            return carry

        lax.fori_loop(1, groups, one, 0)

    def spread(src, dst, ssem, rsem, where, start):
        def one(k, carry):
            peer = lax.rem(me + k, groups)
            pltpu.make_async_remote_copy(
                src_ref=src,
                dst_ref=dst.at[me],
                send_sem=ssem,
                recv_sem=rsem,
                device_id=(where, peer),
                device_id_type=MESH,
            ).start()
            return carry

        lax.fori_loop(start, groups, one, 0)

    lane = lax.broadcasted_iota(jnp.int32, (1, local), 1)
    tile_len = local // blocks.shape[1]
    row_id = lax.broadcasted_iota(jnp.int32, (count, local), 0)
    for m in range(batches):
        for side, index, hot in ((0, senders, send_t), (1, receivers, recv_t)):
            block = jnp.zeros((1, local), jnp.int32)
            for k in range(blocks.shape[1]):
                block = jnp.where(lane // tile_len == k, blocks[m, k, side], block)
            ids = index[m : m + 1, :] + block * 128
            picked = jnp.where(row_id == ids, 1.0, 0.0).astype(F32)
            hot[m] = picked.astype(BF)
            if side == 1:
                recv_1[m] = picked.T.astype(BF)

    def forward(m, carry):
        feats = nodes[m]
        send_feats = lax.dot_general(
            send_t[m], feats, (((0,), (0,)), ((), ())), preferred_element_type=F32
        ).astype(BF)
        recv_feats = dot(recv_1[m], feats).astype(BF)
        pre = dot(send_feats, w_send[...]) + dot(recv_feats, w_recv[...]) + dot(edges[m], w_edge[...])
        sigma = jax.nn.sigmoid(pre)
        done = (pre * sigma).astype(BF)
        act[m] = done
        slope_e[m] = sigma * (1.0 + pre * (1.0 - sigma))
        message = dot(done, w_msg[...]).astype(BF)
        part = dot(recv_t[m], message)
        agg_src[m] = part.astype(BF).reshape(groups, rows, width)

        @pl.when(m == 0)
        def _():
            pl.semaphore_wait(barrier, groups - 1 + groups * (section > 0).astype(jnp.int32))

        scatter(agg_src.at[m], agg_buf.at[m], s_agg.at[m], r_agg.at[m])
        agg_buf[m, me] = agg_src[m, me]
        return carry

    lax.fori_loop(0, batches, forward, 0)

    w_am[...] = lax.dot_general(
        w_agg[...], w_msg[...], (((0,), (1,)), ((), ())), preferred_element_type=F32
    ).astype(BF)

    def gather_aggregate(m, carry):
        take_bytes(agg_buf.at[m, pl.ds(0, groups - 1)], r_agg.at[m])
        summed = jnp.sum(agg_buf[m].astype(F32), axis=0).astype(BF)
        agg_row[m] = summed
        agg_all[m, me] = summed
        spread(agg_row.at[m], agg_all.at[m], s_all.at[m], r_all.at[m], section, 1)
        return carry

    lax.fori_loop(0, batches, gather_aggregate, 0)

    def transposes():
        def one(m, carry):
            nodes_t[m] = nodes[m].T
            edges_t[m] = edges[m].T
            act_t[m] = act[m].T
            return carry

        lax.fori_loop(0, batches, one, 0)

    transposes()
    total[...] = jnp.zeros_like(total)
    for out in (o_node, o_agg, o_out):
        out[...] = jnp.zeros_like(out)

    def backward(m, carry):
        take_bytes(agg_all.at[m, pl.ds(0, groups - 1)], r_all.at[m])
        feats = nodes[m]
        agg_b = agg_all[m].reshape(count, width)
        node_pre = dot(feats, w_node[...]) + dot(agg_b, w_agg[...])
        sigma = jax.nn.sigmoid(node_pre)
        agg_t[...] = agg_b.T
        node_act_t[...] = (node_pre * sigma).astype(BF).T
        slope_n[...] = sigma * (1.0 + node_pre * (1.0 - sigma))

        @pl.when(first)
        def _():
            ge[m] = top_e[m]
            gh[m] = top_n[m].reshape(groups, rows, width)

        @pl.when(section < sections - 1)
        def _():
            take_bytes(ge.at[m], r_ge.at[m])

        base[...] = dot_t(ge[m], w_msg[...])

        @pl.when(section < sections - 1)
        def _():
            take_bytes(gh.at[m], r_gh.at[m])

        grad_nodes = gh[m].reshape(count, width)
        delta = (dot_t(grad_nodes, w_out[...]) * slope_n[...]).astype(BF)
        node_delta[...] = delta
        mixed = dot(delta, w_am[...]).astype(BF)
        edge_delta = ((base[...] + dot(recv_1[m], mixed)) * slope_e[m]).astype(BF)
        at_send = dot(send_t[m], edge_delta).astype(BF)
        at_recv = dot(recv_t[m], edge_delta).astype(BF)
        part = dot_t(at_send, w_send[...]) + dot_t(at_recv, w_recv[...])
        back_src[m] = part.astype(BF).reshape(groups, rows, width)
        scatter(back_src.at[m], back_buf.at[m], s_back.at[m], r_back.at[m])
        back_buf[m, me] = back_src[m, me]

        edge_out[m] = (ge[m].astype(F32) + dot_t(edge_delta, w_edge[...])).astype(BF)

        @pl.when(section > 0)
        def _():
            pltpu.make_async_remote_copy(
                src_ref=edge_out.at[m],
                dst_ref=ge.at[m],
                send_sem=s_ge.at[m],
                recv_sem=r_ge.at[m],
                device_id=(section - 1, me),
                device_id_type=MESH,
            ).start()

        own = node_delta[pl.ds(pl.multiple_of(me * rows, rows), rows), :]
        own_term = gh[m, me].astype(F32) + dot_t(own, w_node[...])

        take_bytes(back_buf.at[m, pl.ds(0, groups - 1)], r_back.at[m])
        summed = (own_term + jnp.sum(back_buf[m].astype(F32), axis=0)).astype(BF)
        node_out[m] = summed
        row_src[m] = summed

        @pl.when(section > 0)
        def _():
            spread(row_src.at[m], gh.at[m], s_gh.at[m], r_gh.at[m], section - 1, 0)

        agg_grad = dot_t(delta, w_agg[...]).astype(BF)
        message_grad = (ge[m].astype(F32) + dot(recv_1[m], agg_grad)).astype(BF)
        total[3] += dot(act_t[m], message_grad)
        total[2] += dot(edges_t[m], edge_delta)
        total[0] += dot(nodes_t[m], at_send)
        total[1] += dot(nodes_t[m], at_recv)
        piece = pl.ds(pl.multiple_of(me * share, share), share)
        o_node[...] += dot(nodes_t[m, piece, :], delta)
        o_agg[...] += dot(agg_t[piece, :], delta)
        o_out[...] += dot(node_act_t[piece, :], grad_nodes)
        return carry

    lax.fori_loop(0, batches, backward, 0)

    outs = (o_send, o_recv, o_edge, o_msg)
    order = (3, 2, 0, 1)
    for i in order:
        grad_src[i] = total[i].astype(BF).reshape(groups, share, width)
        scatter(grad_src.at[i], grad_buf.at[i], s_grad.at[i], r_grad.at[i])
        grad_buf[i, me] = grad_src[i, me]
    for i in order:
        take_bytes(grad_buf.at[i, pl.ds(0, groups - 1)], r_grad.at[i])
        outs[i][...] = jnp.sum(grad_buf[i].astype(F32), axis=0)

    for m in range(batches):
        take_bytes(agg_src.at[m, pl.ds(0, groups - 1)], s_agg.at[m])
        take_bytes(agg_all.at[m, pl.ds(0, groups - 1)], s_all.at[m])
        take_bytes(back_src.at[m, pl.ds(0, groups - 1)], s_back.at[m])

        @pl.when(section > 0)
        def _():
            take_bytes(edge_out.at[m], s_ge.at[m])
            take_bytes(gh.at[m], s_gh.at[m])

    for i in order:
        take_bytes(grad_src.at[i, pl.ds(0, groups - 1)], s_grad.at[i])


def body(sections, groups, *args):
    nodes, edges, top_n, top_e, blocks, senders, receivers, *weights = args
    weights = [w[0] for w in weights]
    nodes, edges = nodes[0], edges[0]
    batches, count, width = nodes.shape
    local = edges.shape[1]
    hidden = weights[0].shape[1]
    rows, share = count // groups, width // groups
    vmem = pl.BlockSpec(memory_space=pltpu.VMEM)
    smem = pl.BlockSpec(memory_space=pltpu.SMEM)
    full = (batches, groups, rows, width)
    sem = pltpu.SemaphoreType.DMA
    scratch = [
        pltpu.VMEM((batches, count, local), BF),
        pltpu.VMEM((batches, count, local), BF),
        pltpu.VMEM((batches, local, count), BF),
        pltpu.VMEM((batches, local, hidden), BF),
        pltpu.VMEM((batches, local, hidden), F32),
        pltpu.VMEM((count, hidden), F32),
        pltpu.VMEM((count, hidden), BF),
        pltpu.VMEM((local, hidden), F32),
        pltpu.VMEM((hidden, hidden), BF),
        pltpu.VMEM((batches, width, count), BF),
        pltpu.VMEM((batches, width, local), BF),
        pltpu.VMEM((batches, hidden, local), BF),
        pltpu.VMEM((width, count), BF),
        pltpu.VMEM((hidden, count), BF),
        pltpu.VMEM((4, width, hidden), F32),
        pltpu.VMEM(full, BF),
        pltpu.VMEM(full, BF),
        pltpu.VMEM((batches, rows, width), BF),
        pltpu.VMEM(full, BF),
        pltpu.VMEM(full, BF),
        pltpu.VMEM(full, BF),
        pltpu.VMEM((batches, rows, width), BF),
        pltpu.VMEM(full, BF),
        pltpu.VMEM((batches, local, width), BF),
        pltpu.VMEM((4, groups, share, hidden), BF),
        pltpu.VMEM((4, groups, share, hidden), BF),
    ] + [sem((batches,))] * 10 + [sem((4,))] * 2
    shapes = [
        jax.ShapeDtypeStruct((batches, rows, width), BF),
        jax.ShapeDtypeStruct((batches, local, width), BF),
    ] + [jax.ShapeDtypeStruct((share, hidden), F32)] * 7
    results = pl.pallas_call(
        functools.partial(kernel, sections, groups),
        out_shape=shapes,
        in_specs=[vmem] * 4 + [smem] + [vmem] * 9,
        out_specs=[vmem] * 9,
        scratch_shapes=scratch,
        compiler_params=pltpu.CompilerParams(
            collective_id=0, has_side_effects=True, vmem_limit_bytes=56 * 1024 * 1024
        ),
        name="window",
    )(nodes, edges, top_n, top_e, blocks, senders, receivers, *weights)
    return tuple(r[None] for r in results)


def solution(mesh):
    in_specs = (
        P("section", None, None, None),
        P("section", None, "edge", None),
        P(),
        P(None, "edge", None),
        P(None, "edge", None),
        P(None, "edge"),
        P(None, "edge"),
    ) + (P("section", None, None),) * 7
    out_specs = (
        P("section", None, "edge", None),
        P("section", None, "edge", None),
    ) + (P("section", "edge", None),) * 7
    step = functools.partial(body, mesh.shape["section"], mesh.shape["edge"])
    return jax.shard_map(step, mesh=mesh, in_specs=in_specs, out_specs=out_specs, check_vma=False)
```

time: 2040 us -> 160 us (0.08)
  waiting for transfers between devices: 946 us -> 0 us
  blocking collectives: 702 us -> 0 us
  matrix products: 214 us -> 0 us
  Pallas kernels: 0 us -> 150 us
  local copies, waits for them, and re-layouts: 123 us -> 9.07 us
  starting transfers between devices: 23.3 us -> 0 us
    psum x9 -> x0, blocking collectives: 702 us -> none  [advance(): aggregate = lax.psum(partial_agg, 'edge')]
    psum x9 -> x0, waiting for transfers between devices: 630 us -> none  [advance(): edge_terms = lax.psum(partial_back, 'edge')]
    reduce_scatter x4 -> x0, waiting for transfers between devices: 302 us -> none  [the longest x1 76.5 us: body(): lax.psum_scatter(sum_msg, 'edge', scatter_dimension=0, tiled=True)]
    dot_general x288 -> x0, matrix products: 214 us -> none  [the longest x63 70.9 us: transposed_times(): lax.dot_general(left, right, (((0,), (0,)), ((), ())), preferred_element_...]
    pallas_call x0 -> x1, Pallas kernels: none -> 150 us  [body(): pl.pallas_call(functools.partial(kernel, sections, groups), out_shape=sha...]
    while x558 -> x0, local copies, waits for them, and re-layouts: 96.3 us -> none
    ppermute x18 -> x0, starting transfers between devices: 23.1 us -> none  [shifted(): return lax.ppermute(shard, axis, pairs)]
  transfers between devices with their start and end apart: 31 -> 0, of which waited for: 22 -> 0; matrix products, arithmetic and copies ran while one was open for 5% -> 0% of each run, Pallas kernels for 0% -> 0%
where the time goes in v1:
time: 160 us; the launch traced here: 159 us
  Pallas kernels  150 us (94%)
  local copies, waits for them, and re-layouts  9.07 us (6%)
    pallas_call x1, Pallas kernels, body(): pl.pallas_call(functools.partial(kernel, sections, groups), out_shape=sha...  150 us
    unnamed x25, local copies, waits for them, and re-layouts  9.07 us

profile of v1, /device:TPU:0, one launch (start us, length us, event | category | flops | bytes accessed | tf_op | source)
XLA Modules:
  0.0 159.4 jit_solution(3361609989262875749)
XLA Ops:
  0.6 149.7 %window.1 = (bf16[2,16,512]{2,1,0:T(8,128)(2,1)}, bf16[2,256,512]{2,1,0:T(8,128)(2,1)}, f32[32,512]{1,0:T(8,128)}, f32[32,512]{1,0:T(8,128)}, f32[32,512]{1,0:T(...) custom-call(bf16[2,256,512]{2,1,0:T(8,128)(2,1)} %bitcast.18, ...), custom_call_target="tpu_custom_call" | custom-call | tf_op jit(solution)/shard_map/window/pallas_call | solution.py:360
  150.3 0.0 copy-start.7
  150.3 0.7 copy-done.7
  151.1 0.6 copy.32
  151.7 0.0 copy-start.6
  151.7 1.9 %copy.33 = bf16[1,2,256,512]{3,2,1,0:T(8,128)(2,1)} copy(bf16[1,2,256,512]{3,2,1,0:T(8,128)(2,1)} %bitcast.27) | data formatting | bytes 1048576
  153.6 0.0 copy-done.6
  153.6 0.0 copy-start.5
  153.6 0.6 copy.34
  154.2 0.2 copy-done.5
  154.4 0.0 copy-start.4
  154.5 0.6 copy.35
  155.1 0.2 copy-done.4
  155.3 0.0 copy-start.3
  155.3 0.6 copy.36
  155.9 0.2 copy-done.3
  156.2 0.0 copy-start.2
  156.2 0.6 copy.37
  156.8 0.2 copy-done.2
  157.0 0.0 copy-start.1
  157.0 0.6 copy.38
  157.7 0.2 copy-done.1
  157.9 0.0 copy-start
  157.9 0.6 copy.39
  158.5 0.2 copy-done
  158.8 0.6 copy.40
Async XLA Ops:
  150.3 0.8 copy-start.7
  151.7 1.9 %copy-start.6 = (f32[32,512]{1,0:T(8,128)S(1)}, f32[32,512]{1,0:T(8,128)}, u32[]{:S(2)}) copy-start(f32[32,512]{1,0:T(8,128)} %get-tuple-element.20) | copy-start | bytes 196612
  153.6 0.9 copy-start.5
  154.4 0.9 copy-start.4
  155.3 0.9 copy-start.3
  156.2 0.9 copy-start.2
  157.0 0.9 copy-start.1
  157.9 0.9 copy-start

commit v2 on v1

v2 whole, which is shorter than its diff:
```python
import functools

import jax
import jax.numpy as jnp
from jax import lax
from jax.experimental import pallas as pl
from jax.experimental.pallas import tpu as pltpu
from jax.sharding import PartitionSpec as P

MESH = pl.DeviceIdType.MESH
BF = jnp.bfloat16
F32 = jnp.float32


def dot(left, right):
    return jnp.dot(left, right, preferred_element_type=F32)


def dot_t(left, right):
    return lax.dot_general(left, right, (((1,), (1,)), ((), ())), preferred_element_type=F32)


def take_bytes(ref, sem):
    pltpu.make_async_copy(ref, ref, sem).wait()


def torus_offsets(side):
    def far(offset):
        return -sum(min(step, side - step) for step in offset)

    return sorted(((a, b) for a in range(side) for b in range(side)), key=far)


def kernel(sections, groups, batches, *refs):
    (
        h_nodes,
        h_edges,
        h_top_n,
        h_top_e,
        blocks,
        senders,
        receivers,
        h_send,
        h_recv,
        h_edge,
        h_msg,
        h_node,
        h_agg,
        h_out,
        h_node_out,
        h_edge_out,
        h_grads,
        nodes,
        edges,
        gh,
        ge,
        w_send,
        w_recv,
        w_edge,
        w_msg,
        w_node,
        w_agg,
        w_out,
        node_out,
        edge_out,
        grads,
        send_t,
        recv_t,
        recv_1,
        act,
        slope_e,
        slope_n,
        node_act,
        node_delta,
        edge_delta,
        at_send,
        at_recv,
        base,
        own_term,
        row_in,
        w_am,
        nodes_t,
        edges_t,
        act_t,
        sum_t,
        agg_t,
        node_act_t,
        agg_b,
        sum_src,
        sum_buf,
        sum_row,
        sum_all,
        back_src,
        back_buf,
        grad_src,
        grad_buf,
        s_load,
        s_store,
        s_sum,
        r_sum,
        s_all,
        r_all,
        s_back,
        r_back,
        s_gh,
        r_gh,
        s_row,
        r_row,
        s_ge,
        r_ge,
        s_grad,
        r_grad,
    ) = refs
    section = lax.axis_index("section")
    me = lax.axis_index("edge")
    count, width = nodes.shape[1:]
    local = edges.shape[1]
    rows = count // groups
    share = width // groups
    side = round(groups**0.5)
    first = section == sections - 1
    hops_down = jnp.logical_and(lax.rem(section, 2) == 0, section > 0)
    relays = jnp.logical_and(lax.rem(section, 2) == 1, section < sections - 1)
    offsets = torus_offsets(side)
    row_at, col_at = me // side, lax.rem(me, side)

    def peer_at(offset):
        return lax.rem(row_at + offset[0], side) * side + lax.rem(col_at + offset[1], side)

    barrier = pltpu.get_barrier_semaphore()
    for offset in offsets[:-1]:
        pl.semaphore_signal(
            barrier, inc=1, device_id=(section, peer_at(offset)), device_id_type=MESH
        )

    @pl.when(section < sections - 1)
    def _():
        for offset in offsets:
            pl.semaphore_signal(
                barrier, inc=1, device_id=(section + 1, peer_at(offset)), device_id_type=MESH
            )

    loads = [
        pltpu.make_async_copy(src, dst, s_load.at[i])
        for i, (src, dst) in enumerate(
            (
                (h_nodes, nodes),
                (h_edges, edges),
                (h_send, w_send),
                (h_recv, w_recv),
                (h_edge, w_edge),
                (h_msg, w_msg),
                (h_node, w_node),
                (h_agg, w_agg),
                (h_out, w_out),
            )
        )
    ]
    for copy in loads:
        copy.start()
    tops = [
        pltpu.make_async_copy(h_top_n, gh, s_load.at[len(loads)]),
        pltpu.make_async_copy(h_top_e, ge, s_load.at[len(loads) + 1]),
    ]

    @pl.when(first)
    def _():
        for copy in tops:
            copy.start()

    def scatter(src, dst, ssem, rsem):
        for offset in offsets[:-1]:
            peer = peer_at(offset)
            pltpu.make_async_remote_copy(
                src_ref=src.at[peer],
                dst_ref=dst.at[me],
                send_sem=ssem,
                recv_sem=rsem,
                device_id=(section, peer),
                device_id_type=MESH,
            ).start()

    def spread(src, dst, ssem, rsem, where, targets):
        for offset in targets:
            pltpu.make_async_remote_copy(
                src_ref=src,
                dst_ref=dst,
                send_sem=ssem,
                recv_sem=rsem,
                device_id=(where, peer_at(offset)),
                device_id_type=MESH,
            ).start()

    lane = lax.broadcasted_iota(jnp.int32, (1, local), 1)
    tile_len = local // blocks.shape[1]
    row_id = lax.broadcasted_iota(jnp.int32, (count, local), 0)
    for m in range(batches):
        for part, index, hot in ((0, senders, send_t), (1, receivers, recv_t)):
            block = jnp.zeros((1, local), jnp.int32)
            for k in range(blocks.shape[1]):
                block = jnp.where(lane // tile_len == k, blocks[m, k, part], block)
            ids = index[m : m + 1, :] + block * 128
            picked = jnp.where(row_id == ids, 1.0, 0.0).astype(F32)
            hot[m] = picked.astype(BF)
            if part == 1:
                recv_1[m] = picked.T.astype(BF)

    for copy in loads[:5]:
        copy.wait()
    mine = pl.ds(pl.multiple_of(me * rows, rows), rows)
    piece = pl.ds(pl.multiple_of(me * share, share), share)

    for m in range(batches):
        feats = nodes[m]
        send_feats = lax.dot_general(
            send_t[m], feats, (((0,), (0,)), ((), ())), preferred_element_type=F32
        ).astype(BF)
        recv_feats = dot(recv_1[m], feats).astype(BF)
        pre = dot(send_feats, w_send[...]) + dot(recv_feats, w_recv[...]) + dot(edges[m], w_edge[...])
        sigma = jax.nn.sigmoid(pre)
        done = (pre * sigma).astype(BF)
        act[m] = done
        slope_e[m] = sigma * (1.0 + pre * (1.0 - sigma))
        sum_src[m] = dot(recv_t[m], done).astype(BF).reshape(groups, rows, width)
        if m == 0:
            pl.semaphore_wait(barrier, groups - 1 + groups * (section > 0).astype(jnp.int32))
        scatter(sum_src.at[m], sum_buf.at[m], s_sum.at[m], r_sum.at[m])
        sum_buf[m, me] = sum_src[m, me]

    for copy in loads[5:]:
        copy.wait()
    w_am[...] = lax.dot_general(
        w_agg[...], w_msg[...], (((0,), (1,)), ((), ())), preferred_element_type=F32
    ).astype(BF)

    for m in range(batches):
        take_bytes(sum_buf.at[m, pl.ds(0, groups - 1)], r_sum.at[m])
        summed = jnp.sum(sum_buf[m].astype(F32), axis=0).astype(BF)
        sum_row[m] = summed
        spread(sum_row.at[m], sum_all.at[m, me], s_all.at[m], r_all.at[m], section, offsets[:-1])
        sum_all[m, me] = summed

    def node_forward(m):
        take_bytes(sum_all.at[m, pl.ds(0, groups - 1)], r_all.at[m])
        agg = dot(sum_all[m].reshape(count, width), w_msg[...]).astype(BF)
        agg_b[m] = agg
        node_pre = dot(nodes[m], w_node[...]) + dot(agg, w_agg[...])
        sigma = jax.nn.sigmoid(node_pre)
        node_act[m] = (node_pre * sigma).astype(BF)
        slope_n[m] = sigma * (1.0 + node_pre * (1.0 - sigma))

    def transposes():
        for m in range(batches):
            at = pl.ds(m * local, local)
            nodes_t[:, m * count : (m + 1) * count] = nodes[m].T
            edges_t[:, at] = edges[m].T
            act_t[:, at] = act[m].T
            sum_t[:, m * count : (m + 1) * count] = sum_all[m].reshape(count, width).T
            agg_t[:, m * count : (m + 1) * count] = agg_b[m].T
            node_act_t[:, m * count : (m + 1) * count] = node_act[m].T

    def edge_base(m):
        base[m] = dot_t(ge[m], w_msg[...])

    def chain(m):
        span = pl.ds(m * local, local)
        at = pl.ds(m * count, count)
        grad_nodes = gh[m].reshape(count, width)
        delta = (dot_t(grad_nodes, w_out[...]) * slope_n[m]).astype(BF)
        node_delta[at, :] = delta
        mixed = dot(delta, w_am[...]).astype(BF)
        moved = ((base[m] + dot(recv_1[m], mixed)) * slope_e[m]).astype(BF)
        edge_delta[span, :] = moved
        to_send = dot(send_t[m], moved).astype(BF)
        to_recv = dot(recv_t[m], moved).astype(BF)
        at_send[at, :] = to_send
        at_recv[at, :] = to_recv
        part = dot_t(to_send, w_send[...]) + dot_t(to_recv, w_recv[...])
        back_src[m] = part.astype(BF).reshape(groups, rows, width)
        scatter(back_src.at[m], back_buf.at[m], s_back.at[m], r_back.at[m])
        back_buf[m, me] = back_src[m, me]

        edge_out[m] = (ge[m].astype(F32) + dot_t(edge_delta[span, :], w_edge[...])).astype(BF)

        @pl.when(section > 0)
        def _():
            pltpu.make_async_remote_copy(
                src_ref=edge_out.at[m],
                dst_ref=ge.at[m],
                send_sem=s_ge.at[m],
                recv_sem=r_ge.at[m],
                device_id=(section - 1, me),
                device_id_type=MESH,
            ).start()

    def own_terms(m):
        own = node_delta[pl.ds(pl.multiple_of(m * count + me * rows, rows), rows), :]
        own_term[m] = gh[m, me].astype(F32) + dot_t(own, w_node[...])

    def finish(m):
        take_bytes(back_buf.at[m, pl.ds(0, groups - 1)], r_back.at[m])
        node_out[m] = (own_term[m] + jnp.sum(back_buf[m].astype(F32), axis=0)).astype(BF)

        @pl.when(lax.rem(section, 2) == 1)
        def _():
            spread(node_out.at[m], gh.at[m, me], s_gh.at[m], r_gh.at[m], section - 1, offsets)

        @pl.when(hops_down)
        def _():
            pltpu.make_async_remote_copy(
                src_ref=node_out.at[m],
                dst_ref=row_in.at[m],
                send_sem=s_row.at[m],
                recv_sem=r_row.at[m],
                device_id=(section - 1, me),
                device_id_type=MESH,
            ).start()

    def relay(m):
        @pl.when(relays)
        def _():
            take_bytes(row_in.at[m], r_row.at[m])
            spread(row_in.at[m], gh.at[m, me], s_gh.at[m], r_gh.at[m], section, offsets[:-1])
            gh[m, me] = row_in[m]

    def take_nodes(m):
        @pl.when(relays)
        def _():
            take_bytes(gh.at[m, pl.ds(0, groups - 1)], r_gh.at[m])

        @pl.when(lax.rem(section, 2) == 0)
        def _():
            take_bytes(gh.at[m], r_gh.at[m])

    def make_grad(i, value):
        grad_src[i] = value.astype(BF).reshape(groups, share, width)

    def send_grad(i):
        scatter(grad_src.at[i], grad_buf.at[i], s_grad.at[i], r_grad.at[i])

    node_forward(0)

    @pl.when(first)
    def _():
        for copy in tops:
            copy.wait()

    @pl.when(section < sections - 1)
    def _():
        node_forward(1)
        transposes()
        take_bytes(ge.at[0], r_ge.at[0])

    edge_base(0)

    @pl.when(section < sections - 1)
    def _():
        relay(0)
        take_bytes(ge.at[1], r_ge.at[1])
        edge_base(1)
        relay(1)
        make_grad(3, dot(act_t[...], ge[...].reshape(batches * local, width)))
        take_nodes(0)

    chain(0)

    @pl.when(first)
    def _():
        node_forward(1)
        edge_base(1)

    @pl.when(section < sections - 1)
    def _():
        take_nodes(1)

    @pl.when(section == 0)
    def _():
        send_grad(3)

    chain(1)

    @pl.when(first)
    def _():
        transposes()
        make_grad(3, dot(act_t[...], ge[...].reshape(batches * local, width)))

    make_grad(2, dot(edges_t[...], edge_delta[...]))

    @pl.when(section == 0)
    def _():
        send_grad(2)

    make_grad(0, dot(nodes_t[...], at_send[...]))

    @pl.when(section == 0)
    def _():
        send_grad(0)

    own_terms(0)
    own_terms(1)

    @pl.when(section > 0)
    def _():
        finish(0)

    make_grad(1, dot(nodes_t[...], at_recv[...]))

    @pl.when(section == 0)
    def _():
        send_grad(1)
        finish(0)

    finish(1)

    @pl.when(section > 0)
    def _():
        for i in (3, 2, 0, 1):
            send_grad(i)

    store_node = pltpu.make_async_copy(node_out, h_node_out, s_store.at[0])
    store_edge = pltpu.make_async_copy(edge_out, h_edge_out, s_store.at[1])
    store_node.start()
    store_edge.start()

    agg_grad = dot_t(node_delta[...], w_agg[...]).astype(BF)
    grads[4] = dot(nodes_t[piece, :], node_delta[...])
    grads[5] = dot(agg_t[piece, :], node_delta[...])
    grads[6] = dot(node_act_t[piece, :], gh[...].reshape(batches * count, width))
    known = dot(sum_t[piece, :], agg_grad)
    for i in (3, 2, 0, 1):
        grad_buf[i, me] = grad_src[i, me]
    for i in (3, 2, 0, 1):
        take_bytes(grad_buf.at[i, pl.ds(0, groups - 1)], r_grad.at[i])
        total = jnp.sum(grad_buf[i].astype(F32), axis=0)
        grads[i] = total + known if i == 3 else total
    store_grads = pltpu.make_async_copy(grads, h_grads, s_store.at[2])
    store_grads.start()

    for m in range(batches):
        take_bytes(sum_src.at[m, pl.ds(0, groups - 1)], s_sum.at[m])
        take_bytes(sum_all.at[m, pl.ds(0, groups - 1)], s_all.at[m])
        take_bytes(back_src.at[m, pl.ds(0, groups - 1)], s_back.at[m])

        @pl.when(section > 0)
        def _():
            take_bytes(edge_out.at[m], s_ge.at[m])

        @pl.when(lax.rem(section, 2) == 1)
        def _():
            take_bytes(gh.at[m], s_gh.at[m])

        @pl.when(hops_down)
        def _():
            take_bytes(row_in.at[m], s_row.at[m])

        @pl.when(relays)
        def _():
            take_bytes(gh.at[m, pl.ds(0, groups - 1)], s_gh.at[m])

    for i in range(4):
        take_bytes(grad_src.at[i, pl.ds(0, groups - 1)], s_grad.at[i])
    store_node.wait()
    store_edge.wait()
    store_grads.wait()


def write_kernel(*refs):
    node_in, edge_in, grads, node_out, edge_out, *outs, sems = refs
    copies = [
        pltpu.make_async_copy(edge_in, edge_out, sems.at[0]),
        pltpu.make_async_copy(node_in, node_out, sems.at[1]),
    ]
    copies += [
        pltpu.make_async_copy(grads.at[i], out, sems.at[2 + i]) for i, out in enumerate(outs)
    ]
    for copy in copies:
        copy.start()
    for copy in copies:
        copy.wait()


def body(sections, groups, *args):
    nodes, edges, top_n, top_e, blocks, senders, receivers, *weights = args
    weights = [w[0] for w in weights]
    nodes, edges = nodes[0], edges[0]
    batches, count, width = nodes.shape
    local = edges.shape[1]
    hidden = weights[0].shape[1]
    rows, share = count // groups, width // groups
    vmem = pl.BlockSpec(memory_space=pltpu.VMEM)
    smem = pl.BlockSpec(memory_space=pltpu.SMEM)
    anyw = pl.BlockSpec(memory_space=pl.ANY)
    full = (batches, groups, rows, width)
    sem = pltpu.SemaphoreType.DMA
    V = pltpu.VMEM
    node_shape = jax.ShapeDtypeStruct((batches, rows, width), BF)
    edge_shape = jax.ShapeDtypeStruct((batches, local, width), BF)
    grad_shape = jax.ShapeDtypeStruct((share, hidden), F32)
    scratch = (
        [V((batches, count, width), BF), V((batches, local, width), BF)]
        + [V(full, BF), V((batches, local, width), BF)]
        + [V(w.shape, BF) for w in weights]
        + [V((batches, rows, width), BF), V((batches, local, width), BF)]
        + [V((7, share, hidden), F32)]
        + [V((batches, count, local), BF), V((batches, count, local), BF)]
        + [V((batches, local, count), BF), V((batches, local, hidden), BF)]
        + [V((batches, local, hidden), F32), V((batches, count, hidden), F32)]
        + [V((batches, count, hidden), BF)]
        + [V((batches * count, hidden), BF), V((batches * local, hidden), BF)]
        + [V((batches * count, hidden), BF), V((batches * count, hidden), BF)]
        + [V((batches, local, hidden), F32), V((batches, rows, width), F32)]
        + [V((batches, rows, width), BF), V((hidden, hidden), BF)]
        + [V((width, batches * count), BF), V((width, batches * local), BF)]
        + [V((hidden, batches * local), BF), V((hidden, batches * count), BF)]
        + [V((width, batches * count), BF), V((hidden, batches * count), BF)]
        + [V((batches, count, width), BF)]
        + [V(full, BF), V(full, BF), V((batches, rows, width), BF), V(full, BF)]
        + [V(full, BF), V(full, BF)]
        + [V((4, groups, share, hidden), BF), V((4, groups, share, hidden), BF)]
        + [sem((11,)), sem((3,))]
        + [sem((batches,))] * 12
        + [sem((4,))] * 2
    )
    node_res, edge_res, grads = pl.pallas_call(
        functools.partial(kernel, sections, groups, batches),
        out_shape=[node_shape, edge_shape, jax.ShapeDtypeStruct((7, share, hidden), F32)],
        in_specs=[anyw] * 4 + [smem] + [vmem] * 2 + [anyw] * 7,
        out_specs=[anyw] * 3,
        scratch_shapes=scratch,
        compiler_params=pltpu.CompilerParams(
            collective_id=0, has_side_effects=True, vmem_limit_bytes=58 * 1024 * 1024
        ),
        name="window",
    )(
        nodes,
        edges,
        top_n.reshape(full),
        top_e,
        blocks,
        senders,
        receivers,
        *weights,
    )
    results = pl.pallas_call(
        write_kernel,
        out_shape=[node_shape, edge_shape] + [grad_shape] * 7,
        in_specs=[vmem] * 3,
        out_specs=[anyw] * 9,
        scratch_shapes=[sem((9,))],
        name="write",
    )(node_res, edge_res, grads)
    return tuple(r[None] for r in results)


def solution(mesh):
    in_specs = (
        P("section", None, None, None),
        P("section", None, "edge", None),
        P(),
        P(None, "edge", None),
        P(None, "edge", None),
        P(None, "edge"),
        P(None, "edge"),
    ) + (P("section", None, None),) * 7
    out_specs = (
        P("section", None, "edge", None),
        P("section", None, "edge", None),
    ) + (P("section", "edge", None),) * 7
    step = functools.partial(body, mesh.shape["section"], mesh.shape["edge"])
    return jax.shard_map(step, mesh=mesh, in_specs=in_specs, out_specs=out_specs, check_vma=False)
```

time: 160 us -> 144 us (0.900)
  local copies, waits for them, and re-layouts: 9.07 us -> 0 us
  Pallas kernels: 150 us -> 143 us
    unnamed x25 -> x0, local copies, waits for them, and re-layouts: 9.07 us -> none
    pallas_call x1 -> x2, Pallas kernels: 150 us -> 143 us  [the longest x1 141 us: body(): pl.pallas_call(functools.partial(kernel, sections, groups, batches), out_...]
where the time goes in v2:
time: 144 us
  Pallas kernels  143 us (99%)
    pallas_call x1, Pallas kernels, body(): pl.pallas_call(functools.partial(kernel, sections, groups, batches), out_...  141 us

profile of v2, /device:TPU:0, one launch (start us, length us, event | category | flops | bytes accessed | tf_op | source)
XLA Modules:
  0.0 144.1 jit_solution(6656085145156542692)
XLA Ops:
  0.6 141.2 %window.1 = (bf16[2,16,512]{2,1,0:T(8,128)(2,1)}, bf16[2,256,512]{2,1,0:T(8,128)(2,1)}, f32[7,32,512]{2,1,0:T(8,128)}) custom-call(bf16[2,256,512]{2,1,0:T(8,128)(2,1)} %bitcast.19, bf16[2,256,512]{2,1,0:T(8,128)(2,1)} %bitcast.20, bf16[2,16,16,512]{3,2,1,0:T(8,128)(2,1)} %bitcast.21, bf16[2,256,512]{2,1,0:T(8,128)(2,1)} %refs_3_.1, s32[2,2,2]{2,1,0:T(2,128)} %refs_4_.1, ...), custom_call_target="tpu_custom_call" | custom-call | tf_op jit(solution)/shard_map/window/pallas_call | solution.py:524
  141.9 2.2 %write.1 = (bf16[2,16,512]{2,1,0:T(8,128)(2,1)}, bf16[2,256,512]{2,1,0:T(8,128)(2,1)}, f32[32,512]{1,0:T(8,128)}, f32[32,512]{1,0:T(8,128)}, f32[32,512]{1,0:T(8...) custom-call(bf16[2,16,512]{2,1,0:T(8,128)(2,1)} %get-tuple-element.21.refs_0_, ...), custom_call_target="tpu_custom_call" | custom-call | tf_op jit(solution)/shard_map/write/pallas_call | solution.py:544

commit v3 on v2

v3 whole, which is shorter than its diff:
```python
import functools

import jax
import jax.numpy as jnp
from jax import lax
from jax.experimental import pallas as pl
from jax.experimental.pallas import tpu as pltpu
from jax.sharding import PartitionSpec as P

MESH = pl.DeviceIdType.MESH
BF = jnp.bfloat16
F32 = jnp.float32


def dot(left, right):
    return jnp.dot(left, right, preferred_element_type=F32)


def dot_t(left, right):
    return lax.dot_general(left, right, (((1,), (1,)), ((), ())), preferred_element_type=F32)


def take_bytes(ref, sem):
    pltpu.make_async_copy(ref, ref, sem).wait()


def torus_offsets(side):
    def far(offset):
        return -sum(min(step, side - step) for step in offset)

    return sorted(((a, b) for a in range(side) for b in range(side)), key=far)


def kernel(sections, groups, batches, *refs):
    (
        h_nodes,
        h_edges,
        h_top_n,
        h_top_e,
        blocks,
        senders,
        receivers,
        h_send,
        h_recv,
        h_edge,
        h_msg,
        h_node,
        h_agg,
        h_out,
        h_node_out,
        h_edge_out,
        h_grads,
        nodes,
        edges,
        gh,
        ge,
        w_send,
        w_recv,
        w_edge,
        w_msg,
        w_node,
        w_agg,
        w_out,
        w_am,
        node_out,
        edge_out,
        grads,
        send_t,
        recv_t,
        recv_1,
        act,
        slope_e,
        slope_n,
        node_act,
        node_delta,
        edge_delta,
        at_send,
        at_recv,
        base,
        own_term,
        row_in,
        nodes_t,
        edges_t,
        act_t,
        sum_t,
        agg_t,
        node_act_t,
        sum_src,
        sum_buf,
        sum_row,
        sum_all,
        back_src,
        back_buf,
        grad_src,
        grad_mid,
        half_src,
        half_buf,
        s_load,
        s_store,
        s_sum,
        r_sum,
        s_all,
        r_all,
        s_back,
        r_back,
        s_gh,
        r_gh,
        s_row,
        r_row,
        s_ge,
        r_ge,
        s_mate,
        r_mate,
        s_grad,
        r_grad,
        s_half,
        r_half,
        turn,
    ) = refs
    section = lax.axis_index("section")
    me = lax.axis_index("edge")
    count, width = nodes.shape[1:]
    local = edges.shape[1]
    rows = count // groups
    share = width // groups
    side = round(groups**0.5)
    odd = lax.rem(section, 2) == 1
    even = lax.rem(section, 2) == 0
    mate = section + 1 - 2 * lax.rem(section, 2)
    first = section == sections - 1
    later = jnp.logical_and(odd, section < sections - 1)
    hands_down = jnp.logical_and(odd, section > 1)
    offsets = torus_offsets(side)
    row_at, col_at = me // side, lax.rem(me, side)

    def peer_at(offset):
        return lax.rem(row_at + offset[0], side) * side + lax.rem(col_at + offset[1], side)

    def remote(src, dst, ssem, rsem, where, peer):
        return pltpu.make_async_remote_copy(
            src_ref=src,
            dst_ref=dst,
            send_sem=ssem,
            recv_sem=rsem,
            device_id=(where, peer),
            device_id_type=MESH,
        )

    barrier = pltpu.get_barrier_semaphore()
    for offset in offsets[:-1]:
        pl.semaphore_signal(
            barrier, inc=1, device_id=(section, peer_at(offset)), device_id_type=MESH
        )
    pl.semaphore_signal(barrier, inc=1, device_id=(mate, me), device_id_type=MESH)

    @pl.when(later)
    def _():
        pl.semaphore_signal(barrier, inc=1, device_id=(section + 2, me), device_id_type=MESH)

    loads = [
        pltpu.make_async_copy(src, dst, s_load.at[i])
        for i, (src, dst) in enumerate(
            (
                (h_nodes, nodes),
                (h_edges, edges),
                (h_send, w_send.at[0]),
                (h_recv, w_recv.at[0]),
                (h_edge, w_edge.at[0]),
                (h_msg, w_msg.at[0]),
                (h_node, w_node.at[0]),
                (h_agg, w_agg),
                (h_out, w_out.at[0]),
            )
        )
    ]
    for copy in loads:
        copy.start()
    tops = [
        pltpu.make_async_copy(h_top_n, gh.at[0], s_load.at[len(loads)]),
        pltpu.make_async_copy(h_top_e, ge, s_load.at[len(loads) + 1]),
    ]

    @pl.when(first)
    def _():
        for copy in tops:
            copy.start()

    def scatter(src, dst, ssem, rsem):
        for offset in offsets[:-1]:
            peer = peer_at(offset)
            remote(src.at[peer], dst.at[me], ssem, rsem, section, peer).start()

    def spread(src, dst, ssem, rsem):
        for offset in offsets[:-1]:
            remote(src, dst, ssem, rsem, section, peer_at(offset)).start()

    def hand(src, dst, i):
        remote(src, dst, s_mate.at[i], r_mate.at[i], mate, me).start()

    lane = lax.broadcasted_iota(jnp.int32, (1, local), 1)
    tile_len = local // blocks.shape[1]
    row_id = lax.broadcasted_iota(jnp.int32, (count, local), 0)
    piece = pl.ds(pl.multiple_of(me * share, share), share)

    for m in range(batches):
        for part, index, hot in ((0, senders, send_t), (1, receivers, recv_t)):
            block = jnp.zeros((1, local), jnp.int32)
            for k in range(blocks.shape[1]):
                block = jnp.where(lane // tile_len == k, blocks[m, k, part], block)
            ids = index[m : m + 1, :] + block * 128
            picked = jnp.where(row_id == ids, 1.0, 0.0).astype(F32)
            hot[m] = picked.astype(BF)
            if part == 1:
                recv_1[m] = picked.T.astype(BF)
        if m == 0:
            for copy in loads[:5]:
                copy.wait()
        feats = nodes[m]
        send_feats = lax.dot_general(
            send_t[m], feats, (((0,), (0,)), ((), ())), preferred_element_type=F32
        ).astype(BF)
        recv_feats = dot(recv_1[m], feats).astype(BF)
        pre = (
            dot(send_feats, w_send[0]) + dot(recv_feats, w_recv[0]) + dot(edges[m], w_edge[0])
        )
        sigma = jax.nn.sigmoid(pre)
        done = (pre * sigma).astype(BF)
        act[m] = done
        slope_e[0, m] = sigma * (1.0 + pre * (1.0 - sigma))
        sum_src[m] = dot(recv_t[m], done).astype(BF).reshape(groups, rows, width)
        if m == 0:
            pl.semaphore_wait(barrier, groups + hands_down.astype(jnp.int32))
        sum_buf[m, me] = sum_src[m, me]

        @pl.when(odd)
        def _():
            scatter(sum_src.at[m], sum_buf.at[m], s_sum.at[m], r_sum.at[m])

    for copy in loads[5:]:
        copy.wait()
    w_am[0] = lax.dot_general(
        w_agg[...], w_msg[0], (((0,), (1,)), ((), ())), preferred_element_type=F32
    ).astype(BF)
    down = (w_msg, w_send, w_recv, w_edge, w_node, w_out, w_am)

    @pl.when(even)
    def _():
        for i, w in enumerate(down):
            hand(w.at[0], w.at[1], i)
        for m in range(batches):
            hand(slope_e.at[0, m], slope_e.at[1, m], 7 + m)
        pl.semaphore_wait(turn, 1)
        for m in range(batches):
            scatter(sum_src.at[m], sum_buf.at[m], s_sum.at[m], r_sum.at[m])

    for m in range(batches):
        slope_n[0, m] = dot(nodes[m], w_node[0])

    @pl.when(first)
    def _():
        for copy in tops:
            copy.wait()
        for m in range(batches):
            base[m] = dot_t(ge[m], w_msg[0])

    for m in range(batches):
        take_bytes(sum_buf.at[m, pl.ds(0, groups - 1)], r_sum.at[m])
        summed = jnp.sum(sum_buf[m].astype(F32), axis=0).astype(BF)
        sum_row[m] = summed
        spread(sum_row.at[m], sum_all.at[m, me], s_all.at[m], r_all.at[m])
        sum_all[m, me] = summed

    @pl.when(odd)
    def _():
        pl.semaphore_signal(turn, inc=1, device_id=(mate, me), device_id_type=MESH)

    def node_forward(m):
        take_bytes(sum_all.at[m, pl.ds(0, groups - 1)], r_all.at[m])
        node_pre = slope_n[0, m] + dot_t(sum_all[m].reshape(count, width), w_am[0])
        sigma = jax.nn.sigmoid(node_pre)
        node_act[m] = (node_pre * sigma).astype(BF)
        slope_n[0, m] = sigma * (1.0 + node_pre * (1.0 - sigma))

        @pl.when(even)
        def _():
            hand(slope_n.at[0, m], slope_n.at[1, m], 9 + m)

    def transposes():
        for m in range(batches):
            at = pl.ds(m * local, local)
            nodes_t[:, m * count : (m + 1) * count] = nodes[m].T
            edges_t[:, at] = edges[m].T
            act_t[:, at] = act[m].T
            sum_t[:, m * count : (m + 1) * count] = sum_all[m].reshape(count, width).T
            agg = dot(sum_all[m].reshape(count, width), w_msg[0]).astype(BF)
            agg_t[:, m * count : (m + 1) * count] = agg.T
            node_act_t[:, m * count : (m + 1) * count] = node_act[m].T

    def edge_grad(li, m):
        return ge[m] if li == 0 else edge_out[0, m]

    def edge_base(li, m):
        base[m] = dot_t(edge_grad(li, m), w_msg[li])

    def chain(li, m):
        slot = li * batches + m
        span = pl.ds(m * local, local)
        at = pl.ds(m * count, count)
        grad_nodes = gh[li, m].reshape(count, width)
        delta = (dot_t(grad_nodes, w_out[li]) * slope_n[li, m]).astype(BF)
        node_delta[li, at, :] = delta
        mixed = dot(delta, w_am[li]).astype(BF)
        moved = ((base[m] + dot(recv_1[m], mixed)) * slope_e[li, m]).astype(BF)
        edge_delta[li, span, :] = moved
        if li == 1:

            @pl.when(section == 1)
            def _():
                hand(edge_delta.at[1, span], edge_delta.at[0, span], 2 + m)

        to_send = dot(send_t[m], moved).astype(BF)
        to_recv = dot(recv_t[m], moved).astype(BF)
        at_send[li, at, :] = to_send
        at_recv[li, at, :] = to_recv
        part = dot_t(to_send, w_send[li]) + dot_t(to_recv, w_recv[li])
        back_src[slot] = part.astype(BF).reshape(groups, rows, width)
        scatter(back_src.at[slot], back_buf.at[slot], s_back.at[slot], r_back.at[slot])
        back_buf[slot, me] = back_src[slot, me]
        if li == 1:

            @pl.when(section == 1)
            def _():
                hand_rest(m)

        edge_out[li, m] = (
            edge_grad(li, m).astype(F32) + dot_t(edge_delta[li, span, :], w_edge[li])
        ).astype(BF)
        if li == 0:
            hand(edge_out.at[0, m], ge.at[m], m)
        elif m == 0:

            @pl.when(section > 1)
            def _():
                edges_down(m)

    def hand_rest(m):
        at = pl.ds(m * count, count)
        hand(at_send.at[1, at], at_send.at[0, at], 4 + m)
        hand(at_recv.at[1, at], at_recv.at[0, at], 6 + m)
        hand(node_delta.at[1, at], node_delta.at[0, at], 8 + m)
        hand(gh.at[1, m], gh.at[0, m], 10 + m)

    def edges_down(m):
        remote(edge_out.at[1, m], ge.at[m], s_ge.at[m], r_ge.at[m], section - 2, me).start()

    def own_terms(li, m):
        own = node_delta[li, pl.ds(pl.multiple_of(m * count + me * rows, rows), rows), :]
        own_term[m] = gh[li, m, me].astype(F32) + dot_t(own, w_node[li])

    def finish(li, m):
        slot = li * batches + m
        take_bytes(back_buf.at[slot, pl.ds(0, groups - 1)], r_back.at[slot])
        summed = (own_term[m] + jnp.sum(back_buf[slot].astype(F32), axis=0)).astype(BF)
        node_out[li, m] = summed
        if li == 0:
            spread(node_out.at[0, m], gh.at[1, m, me], s_gh.at[2 + m], r_gh.at[2 + m])
            gh[1, m, me] = summed
        else:

            @pl.when(section > 1)
            def _():
                remote(
                    node_out.at[1, m], row_in.at[m], s_row.at[m], r_row.at[m], section - 2, me
                ).start()

            hand(node_out.at[1, m], node_out.at[0, m], 12 + m)

    def relay(m):
        take_bytes(row_in.at[m], r_row.at[m])
        spread(row_in.at[m], gh.at[0, m, me], s_gh.at[m], r_gh.at[m])
        gh[0, m, me] = row_in[m]

    def take_nodes(li, m):
        take_bytes(gh.at[li, m, pl.ds(0, groups - 1)], r_gh.at[li * batches + m])

    def make_grad(i):
        if i == 3:
            value = dot(act_t[...], ge[...].reshape(batches * local, width))
        elif i == 2:
            value = dot(edges_t[...], edge_delta[0])
        else:
            value = dot(nodes_t[...], (at_send if i == 0 else at_recv)[0])
        value = value.astype(BF)
        wide = width // 2
        left = value[:, :wide].reshape(side, side, share, wide)
        for k in range(side):
            grad_src[2 * i, k] = left[:, k]
        grad_src[2 * i + 1] = value[:, wide:].reshape(side, side, share, wide)

    steps = sorted(range(1, side), key=lambda step: -min(step, side - step))

    def along(half, step):
        return lax.rem((row_at if half else col_at) + step, side)

    def peer_along(half, spot):
        return spot * side + col_at if half else row_at * side + spot

    def send_grad(i):
        for half in range(2):
            slot = 2 * i + half
            for step in steps:
                spot = along(half, step)
                remote(
                    grad_src.at[slot, spot],
                    grad_mid.at[slot, along(half, 0)],
                    s_grad.at[slot],
                    r_grad.at[slot],
                    section,
                    peer_along(half, spot),
                ).start()

    def pass_grad(i):
        for half in range(2):
            slot = 2 * i + half
            here = along(half, 0)
            grad_mid[slot, here] = grad_src[slot, here]
            take_bytes(grad_mid.at[slot, pl.ds(0, side - 1)], r_grad.at[slot])
            half_src[slot] = jnp.sum(grad_mid[slot].astype(F32), axis=0).astype(BF)
            for step in steps:
                spot = along(1 - half, step)
                remote(
                    half_src.at[slot, spot],
                    half_buf.at[slot, along(1 - half, 0)],
                    s_half.at[slot],
                    r_half.at[slot],
                    section,
                    peer_along(1 - half, spot),
                ).start()
            half_buf[slot, along(1 - half, 0)] = half_src[slot, along(1 - half, 0)]

    node_forward(0)

    @pl.when(section < sections - 1)
    def _():
        node_forward(1)
        transposes()

    @pl.when(odd)
    def _():
        @pl.when(later)
        def _():
            take_bytes(ge.at[0], r_ge.at[0])
            edge_base(0, 0)
            relay(0)
            relay(1)
            take_nodes(0, 0)

        chain(0, 0)

        @pl.when(first)
        def _():
            node_forward(1)

        @pl.when(later)
        def _():
            take_bytes(ge.at[1], r_ge.at[1])
            edge_base(0, 1)
            take_nodes(0, 1)

        chain(0, 1)
        own_terms(0, 0)
        own_terms(0, 1)
        for i, w in enumerate(down):
            take_bytes(w.at[1], r_mate.at[i])
        edge_base(1, 0)
        edge_base(1, 1)
        finish(0, 0)
        finish(0, 1)

        @pl.when(first)
        def _():
            transposes()

        for i in (3, 2, 0, 1):
            make_grad(i)

            @pl.when(section == 1)
            def _():
                send_grad(i)

        for m in range(batches):
            take_bytes(slope_e.at[1, m], r_mate.at[7 + m])
            take_bytes(slope_n.at[1, m], r_mate.at[9 + m])
        take_nodes(1, 0)
        chain(1, 0)
        take_nodes(1, 1)
        chain(1, 1)
        own_terms(1, 0)
        own_terms(1, 1)
        finish(1, 0)

        @pl.when(section > 1)
        def _():
            edges_down(1)

        finish(1, 1)

        @pl.when(section > 1)
        def _():
            for m in range(batches):
                span = pl.ds(m * local, local)
                hand(edge_delta.at[1, span], edge_delta.at[0, span], 2 + m)
                hand_rest(m)

        for m in range(batches):
            hand(edge_out.at[1, m], edge_out.at[0, m], 14 + m)

        @pl.when(section > 1)
        def _():
            for i in (3, 2, 0, 1):
                send_grad(i)

    def take_outs():
        for m in range(batches):
            take_bytes(node_out.at[0, m], r_mate.at[12 + m])
            take_bytes(edge_out.at[0, m], r_mate.at[14 + m])

    @pl.when(even)
    def _():
        for m in range(batches):
            take_bytes(ge.at[m], r_mate.at[m])
        make_grad(3)
        last = section == 0
        for i, ref, at in ((2, edge_delta, 2), (0, at_send, 4), (1, at_recv, 6)):
            for m in range(batches):
                take_bytes(ref.at[0, pl.ds(m * local, local)], r_mate.at[at + m])
                if i == 2 and m == 0:

                    @pl.when(last)
                    def _():
                        send_grad(3)

            make_grad(i)

            @pl.when(last)
            def _():
                send_grad(i)

        for m in range(batches):
            take_bytes(node_delta.at[0, pl.ds(m * count, count)], r_mate.at[8 + m])
            take_bytes(gh.at[0, m], r_mate.at[10 + m])

        @pl.when(section > 0)
        def _():
            take_outs()
            for i in (3, 2, 0, 1):
                send_grad(i)

    agg_grad = dot_t(node_delta[0], w_agg[...]).astype(BF)
    grads[4] = dot(nodes_t[piece, :], node_delta[0])
    grads[5] = dot(agg_t[piece, :], node_delta[0])
    grads[6] = dot(node_act_t[piece, :], gh[0].reshape(batches * count, width))
    known = dot(sum_t[piece, :], agg_grad)
    for i in (3, 2, 0, 1):
        pass_grad(i)

    @pl.when(section == 0)
    def _():
        take_outs()

    store_node = pltpu.make_async_copy(node_out.at[0], h_node_out, s_store.at[0])
    store_edge = pltpu.make_async_copy(edge_out.at[0], h_edge_out, s_store.at[1])
    store_node.start()
    store_edge.start()
    for i in (3, 2, 0, 1):
        for half in range(2):
            slot = 2 * i + half
            lanes = slice(half * (width // 2), (half + 1) * (width // 2))
            take_bytes(half_buf.at[slot, pl.ds(0, side - 1)], r_half.at[slot])
            total = jnp.sum(half_buf[slot].astype(F32), axis=0)
            grads[i, :, lanes] = total + known[:, lanes] if i == 3 else total
    store_grads = pltpu.make_async_copy(grads, h_grads, s_store.at[2])
    store_grads.start()

    for m in range(batches):
        take_bytes(sum_src.at[m, pl.ds(0, groups - 1)], s_sum.at[m])
        take_bytes(sum_all.at[m, pl.ds(0, groups - 1)], s_all.at[m])

    @pl.when(even)
    def _():
        for i, w in enumerate(down):
            take_bytes(w.at[0], s_mate.at[i])
        for m in range(batches):
            take_bytes(slope_e.at[0, m], s_mate.at[7 + m])
            take_bytes(slope_n.at[0, m], s_mate.at[9 + m])

    @pl.when(odd)
    def _():
        for m in range(batches):
            for li in range(2):
                slot = li * batches + m
                take_bytes(back_src.at[slot, pl.ds(0, groups - 1)], s_back.at[slot])
            take_bytes(gh.at[1, m, pl.ds(0, groups - 1)], s_gh.at[2 + m])
            take_bytes(ge.at[m], s_mate.at[m])
            for ref, at in ((edge_delta, 2), (at_send, 4), (at_recv, 6), (node_delta, 8)):
                take_bytes(ref.at[1, pl.ds(m * local, local)], s_mate.at[at + m])
            take_bytes(gh.at[1, m], s_mate.at[10 + m])
            take_bytes(node_out.at[1, m], s_mate.at[12 + m])
            take_bytes(edge_out.at[1, m], s_mate.at[14 + m])

        @pl.when(section > 1)
        def _():
            for m in range(batches):
                take_bytes(row_in.at[m], s_row.at[m])
                take_bytes(ge.at[m], s_ge.at[m])

        @pl.when(later)
        def _():
            for m in range(batches):
                take_bytes(gh.at[0, m, pl.ds(0, groups - 1)], s_gh.at[m])

    for slot in range(8):
        take_bytes(grad_src.at[slot, pl.ds(0, side - 1)], s_grad.at[slot])
        take_bytes(half_src.at[slot, pl.ds(0, side - 1)], s_half.at[slot])
    store_node.wait()
    store_edge.wait()
    store_grads.wait()


def write_kernel(*refs):
    node_in, edge_in, grads, node_out, edge_out, *outs = refs[:-5]
    node_at, edge_at, grad_at, sem_in, sem_out = refs[-5:]
    moves = [(edge_in.at[m], edge_at.at[m], edge_out.at[m]) for m in range(edge_in.shape[0])]
    moves += [(node_in, node_at, node_out)]
    moves += [(grads.at[i], grad_at.at[i], out) for i, out in enumerate(outs)]
    ins = [pltpu.make_async_copy(a, b, sem_in.at[i]) for i, (a, b, _) in enumerate(moves)]
    outs = [pltpu.make_async_copy(b, c, sem_out.at[i]) for i, (_, b, c) in enumerate(moves)]
    for copy in ins:
        copy.start()
    for copy, after in zip(ins, outs):
        copy.wait()
        after.start()
    for copy in outs:
        copy.wait()


def body(sections, groups, *args):
    nodes, edges, top_n, top_e, blocks, senders, receivers, *weights = args
    weights = [w[0] for w in weights]
    nodes, edges = nodes[0], edges[0]
    batches, count, width = nodes.shape
    local = edges.shape[1]
    hidden = weights[0].shape[1]
    rows, share = count // groups, width // groups
    vmem = pl.BlockSpec(memory_space=pltpu.VMEM)
    smem = pl.BlockSpec(memory_space=pltpu.SMEM)
    anyw = pl.BlockSpec(memory_space=pl.ANY)
    full = (batches, groups, rows, width)
    sem = pltpu.SemaphoreType.DMA
    V = pltpu.VMEM
    node_shape = jax.ShapeDtypeStruct((batches, rows, width), BF)
    edge_shape = jax.ShapeDtypeStruct((batches, local, width), BF)
    grad_shape = jax.ShapeDtypeStruct((share, hidden), F32)
    pair = (2, batches)
    side = round(groups**0.5)
    scratch = (
        [V((batches, count, width), BF), V((batches, local, width), BF)]
        + [V((2,) + full, BF), V((batches, local, width), BF)]
        + [V(w.shape if i == 5 else (2,) + w.shape, BF) for i, w in enumerate(weights)]
        + [V((2, hidden, hidden), BF)]
        + [V(pair + (rows, width), BF), V(pair + (local, width), BF)]
        + [V((7, share, hidden), F32)]
        + [V((batches, count, local), BF), V((batches, count, local), BF)]
        + [V((batches, local, count), BF), V((batches, local, hidden), BF)]
        + [V(pair + (local, hidden), F32), V(pair + (count, hidden), F32)]
        + [V((batches, count, hidden), BF)]
        + [V((2, batches * count, hidden), BF), V((2, batches * local, hidden), BF)]
        + [V((2, batches * count, hidden), BF), V((2, batches * count, hidden), BF)]
        + [V((batches, local, hidden), F32), V((batches, rows, width), F32)]
        + [V((batches, rows, width), BF)]
        + [V((width, batches * count), BF), V((width, batches * local), BF)]
        + [V((hidden, batches * local), BF), V((hidden, batches * count), BF)]
        + [V((width, batches * count), BF), V((hidden, batches * count), BF)]
        + [V(full, BF), V(full, BF), V((batches, rows, width), BF), V(full, BF)]
        + [V((2 * batches,) + full[1:], BF), V((2 * batches,) + full[1:], BF)]
        + [V((8, side, side, share, hidden // 2), BF)] * 2
        + [V((8, side, share, hidden // 2), BF)] * 2
        + [sem((11,)), sem((3,))]
        + [sem((batches,))] * 4
        + [sem((2 * batches,))] * 4
        + [sem((batches,))] * 4
        + [sem((16,))] * 2
        + [sem((8,))] * 4
        + [pltpu.SemaphoreType.REGULAR]
    )
    node_res, edge_res, grads = pl.pallas_call(
        functools.partial(kernel, sections, groups, batches),
        out_shape=[node_shape, edge_shape, jax.ShapeDtypeStruct((7, share, hidden), F32)],
        in_specs=[anyw] * 4 + [smem] + [vmem] * 2 + [anyw] * 7,
        out_specs=[anyw] * 3,
        scratch_shapes=scratch,
        compiler_params=pltpu.CompilerParams(
            collective_id=0, has_side_effects=True, vmem_limit_bytes=58 * 1024 * 1024
        ),
        name="window",
    )(
        nodes,
        edges,
        top_n.reshape(full),
        top_e,
        blocks,
        senders,
        receivers,
        *weights,
    )
    results = pl.pallas_call(
        write_kernel,
        out_shape=[node_shape, edge_shape] + [grad_shape] * 7,
        in_specs=[anyw] * 3,
        out_specs=[anyw] * 9,
        scratch_shapes=[
            V(node_shape.shape, BF),
            V(edge_shape.shape, BF),
            V((7, share, hidden), F32),
            sem((batches + 8,)),
            sem((batches + 8,)),
        ],
        name="write",
    )(node_res, edge_res, grads)
    return tuple(r[None] for r in results)


def solution(mesh):
    in_specs = (
        P("section", None, None, None),
        P("section", None, "edge", None),
        P(),
        P(None, "edge", None),
        P(None, "edge", None),
        P(None, "edge"),
        P(None, "edge"),
    ) + (P("section", None, None),) * 7
    out_specs = (
        P("section", None, "edge", None),
        P("section", None, "edge", None),
    ) + (P("section", "edge", None),) * 7
    step = functools.partial(body, mesh.shape["section"], mesh.shape["edge"])
    return jax.shard_map(step, mesh=mesh, in_specs=in_specs, out_specs=out_specs, check_vma=False)
```

time: 144 us -> 127 us (0.88); the launches traced: 144 us -> 125 us
  Pallas kernels: 143 us -> 124 us
    pallas_call x1, Pallas kernels: 141 us -> 122 us  [body(): pl.pallas_call(functools.partial(kernel, sections, groups, batches), out_...]
where the time goes in v3:
time: 127 us; the launch traced here: 125 us
  Pallas kernels  124 us (98%)
    pallas_call x1, Pallas kernels, body(): pl.pallas_call(functools.partial(kernel, sections, groups, batches), out_...  122 us

profile of v3, /device:TPU:0, one launch (start us, length us, event | category | flops | bytes accessed | tf_op | source)
XLA Modules:
  0.0 125.2 jit_solution(7734790240257058131)
XLA Ops:
  0.6 122.3 %window.1 = (bf16[2,16,512]{2,1,0:T(8,128)(2,1)}, bf16[2,256,512]{2,1,0:T(8,128)(2,1)}, f32[7,32,512]{2,1,0:T(8,128)}) custom-call(bf16[2,256,512]{2,1,0:T(8,128)(2,1)} %bitcast.19, bf16[2,256,512]{2,1,0:T(8,128)(2,1)} %bitcast.20, bf16[2,16,16,512]{3,2,1,0:T(8,128)(2,1)} %bitcast.21, bf16[2,256,512]{2,1,0:T(8,128)(2,1)} %refs_3_.1, s32[2,2,2]{2,1,0:T(2,128)} %refs_4_.1, ...), custom_call_target="tpu_custom_call" | custom-call | tf_op jit(solution)/shard_map/window/pallas_call | solution.py:696
  123.0 2.1 %write.1 = (bf16[2,16,512]{2,1,0:T(8,128)(2,1)}, bf16[2,256,512]{2,1,0:T(8,128)(2,1)}, f32[32,512]{1,0:T(8,128)}, f32[32,512]{1,0:T(8,128)}, f32[32,512]{1,0:T(8...) custom-call(bf16[2,16,512]{2,1,0:T(8,128)(2,1)} %get-tuple-element.21.refs_0_, ...), custom_call_target="tpu_custom_call" | custom-call | tf_op jit(solution)/shard_map/write/pallas_call | solution.py:716

commit v4 on v3

--- a/solution.py
+++ b/solution.py
@@ -173,17 +173,13 @@
             )
         )
     ]
-    for copy in loads:
+    for copy in loads[:5]:
         copy.start()
     tops = [
         pltpu.make_async_copy(h_top_n, gh.at[0], s_load.at[len(loads)]),
         pltpu.make_async_copy(h_top_e, ge, s_load.at[len(loads) + 1]),
     ]
 
-    @pl.when(first)
-    def _():
-        for copy in tops:
-            copy.start()
 
     def scatter(src, dst, ssem, rsem):
         for offset in offsets[:-1]:
@@ -215,6 +211,14 @@
         if m == 0:
             for copy in loads[:5]:
                 copy.wait()
+            for copy in loads[5:]:
+                copy.start()
+
+            @pl.when(first)
+            def _():
+                for copy in tops:
+                    copy.start()
+
         feats = nodes[m]
         send_feats = lax.dot_general(
             send_t[m], feats, (((0,), (0,)), ((), ())), preferred_element_type=F32
@@ -235,6 +239,8 @@
         @pl.when(odd)
         def _():
             scatter(sum_src.at[m], sum_buf.at[m], s_sum.at[m], r_sum.at[m])
+            if m == batches - 1:
+                pl.semaphore_signal(turn, inc=1, device_id=(mate, me), device_id_type=MESH)
 
     for copy in loads[5:]:
         copy.wait()
@@ -269,10 +275,6 @@
         sum_row[m] = summed
         spread(sum_row.at[m], sum_all.at[m, me], s_all.at[m], r_all.at[m])
         sum_all[m, me] = summed
-
-    @pl.when(odd)
-    def _():
-        pl.semaphore_signal(turn, inc=1, device_id=(mate, me), device_id_type=MESH)
 
     def node_forward(m):
         take_bytes(sum_all.at[m, pl.ds(0, groups - 1)], r_all.at[m])
@@ -470,23 +472,45 @@
         chain(0, 1)
         own_terms(0, 0)
         own_terms(0, 1)
+
+        @pl.when(later)
+        def _():
+            for i in (2, 3):
+                make_grad(i)
+
+                @pl.when(section == 1)
+                def _():
+                    send_grad(i)
+
+        finish(0, 0)
+        finish(0, 1)
+
+        @pl.when(later)
+        def _():
+            make_grad(0)
+
+            @pl.when(section == 1)
+            def _():
+                send_grad(0)
+
         for i, w in enumerate(down):
             take_bytes(w.at[1], r_mate.at[i])
         edge_base(1, 0)
         edge_base(1, 1)
-        finish(0, 0)
-        finish(0, 1)
 
         @pl.when(first)
         def _():
             transposes()
-
-        for i in (3, 2, 0, 1):
-            make_grad(i)
-
-            @pl.when(section == 1)
-            def _():
-                send_grad(i)
+            for i in (3, 2, 0):
+                make_grad(i)
+
+        make_grad(1)
+
+        @pl.when(section == 1)
+        def _():
+            send_grad(1)
+            pass_grad(2)
+            pass_grad(3)
 
         for m in range(batches):
             take_bytes(slope_e.at[1, m], r_mate.at[7 + m])
@@ -561,8 +585,13 @@
     grads[5] = dot(agg_t[piece, :], node_delta[0])
     grads[6] = dot(node_act_t[piece, :], gh[0].reshape(batches * count, width))
     known = dot(sum_t[piece, :], agg_grad)
-    for i in (3, 2, 0, 1):
-        pass_grad(i)
+    @pl.when(section != 1)
+    def _():
+        pass_grad(3)
+        pass_grad(2)
+
+    pass_grad(0)
+    pass_grad(1)
 
     @pl.when(section == 0)
     def _():

time: 127 us -> 122 us (0.961); the launches traced: 125 us -> 122 us
  Pallas kernels: 124 us -> 121 us
    pallas_call x1, Pallas kernels: 122 us -> 119 us  [body(): pl.pallas_call(functools.partial(kernel, sections, groups, batches), out_...]
where the time goes in v4:
time: 122 us
  Pallas kernels  121 us (99%)
    pallas_call x1, Pallas kernels, body(): pl.pallas_call(functools.partial(kernel, sections, groups, batches), out_...  119 us

profile of v4, /device:TPU:0, one launch (start us, length us, event | category | flops | bytes accessed | tf_op | source)
XLA Modules:
  0.0 122.0 jit_solution(17066168177591040788)
XLA Ops:
  0.6 119.1 %window.1 = (bf16[2,16,512]{2,1,0:T(8,128)(2,1)}, bf16[2,256,512]{2,1,0:T(8,128)(2,1)}, f32[7,32,512]{2,1,0:T(8,128)}) custom-call(bf16[2,256,512]{2,1,0:T(8,128)(2,1)} %bitcast.19, bf16[2,256,512]{2,1,0:T(8,128)(2,1)} %bitcast.20, bf16[2,16,16,512]{3,2,1,0:T(8,128)(2,1)} %bitcast.21, bf16[2,256,512]{2,1,0:T(8,128)(2,1)} %refs_3_.1, s32[2,2,2]{2,1,0:T(2,128)} %refs_4_.1, ...), custom_call_target="tpu_custom_call" | custom-call | tf_op jit(solution)/shard_map/window/pallas_call | solution.py:725
  119.8 2.1 %write.1 = (bf16[2,16,512]{2,1,0:T(8,128)(2,1)}, bf16[2,256,512]{2,1,0:T(8,128)(2,1)}, f32[32,512]{1,0:T(8,128)}, f32[32,512]{1,0:T(8,128)}, f32[32,512]{1,0:T(8...) custom-call(bf16[2,16,512]{2,1,0:T(8,128)(2,1)} %get-tuple-element.21.refs_0_, ...), custom_call_target="tpu_custom_call" | custom-call | tf_op jit(solution)/shard_map/write/pallas_call | solution.py:745

commit v5 on v4

--- a/solution.py
+++ b/solution.py
@@ -498,13 +498,9 @@
         edge_base(1, 0)
         edge_base(1, 1)
 
-        @pl.when(first)
-        def _():
-            transposes()
-            for i in (3, 2, 0):
-                make_grad(i)
-
-        make_grad(1)
+        @pl.when(later)
+        def _():
+            make_grad(1)
 
         @pl.when(section == 1)
         def _():
@@ -538,6 +534,12 @@
 
         for m in range(batches):
             hand(edge_out.at[1, m], edge_out.at[0, m], 14 + m)
+
+        @pl.when(first)
+        def _():
+            transposes()
+            for i in (3, 2, 0, 1):
+                make_grad(i)
 
         @pl.when(section > 1)
         def _():

time: 122 us -> 122 us (level)
  no operation moved by 1% of the time
where the time goes in v5:
time: 122 us; the launch traced here: 121 us
  Pallas kernels  120 us (98%)
    pallas_call x1, Pallas kernels, body(): pl.pallas_call(functools.partial(kernel, sections, groups, batches), out_...  118 us

profile of v5, /device:TPU:0, one launch (start us, length us, event | category | flops | bytes accessed | tf_op | source)
XLA Modules:
  0.0 121.3 jit_solution(13015689018940257555)
XLA Ops:
  0.6 118.4 %window.1 = (bf16[2,16,512]{2,1,0:T(8,128)(2,1)}, bf16[2,256,512]{2,1,0:T(8,128)(2,1)}, f32[7,32,512]{2,1,0:T(8,128)}) custom-call(bf16[2,256,512]{2,1,0:T(8,128)(2,1)} %bitcast.19, bf16[2,256,512]{2,1,0:T(8,128)(2,1)} %bitcast.20, bf16[2,16,16,512]{3,2,1,0:T(8,128)(2,1)} %bitcast.21, bf16[2,256,512]{2,1,0:T(8,128)(2,1)} %refs_3_.1, s32[2,2,2]{2,1,0:T(2,128)} %refs_4_.1, ...), custom_call_target="tpu_custom_call" | custom-call | tf_op jit(solution)/shard_map/window/pallas_call | solution.py:727
  119.1 2.1 %write.1 = (bf16[2,16,512]{2,1,0:T(8,128)(2,1)}, bf16[2,256,512]{2,1,0:T(8,128)(2,1)}, f32[32,512]{1,0:T(8,128)}, f32[32,512]{1,0:T(8,128)}, f32[32,512]{1,0:T(8...) custom-call(bf16[2,16,512]{2,1,0:T(8,128)(2,1)} %get-tuple-element.21.refs_0_, ...), custom_call_target="tpu_custom_call" | custom-call | tf_op jit(solution)/shard_map/write/pallas_call | solution.py:747
